TPU v7x, 512 devices: a whole 4x8x8 slice. The times are simulated.
512 devices in a mesh: mom: 128 (over y, z, core), tm: 4 (over x).
Axes of the slice: x: 4, y: 8, z: 8, core: 2. Of those that a mesh axis runs over, the one named last changes fastest.
Arguments:
- history: float32 [4, 128, 640, 1024], P(None, 'mom', None, 'tm'), may hold values from -6 to 6
- sigma_first: float32 [4, 128, 1024], P(None, None, 'tm'), may hold values from -4 to 4
- propagator: float32 [4, 128, 384], P(None, 'mom'), may hold values from -4 to 4
Outputs:
- green_last: float32 [4, 128, 128, 1024], P(None, 'mom', None, 'tm')
- sigma_next: float32 [4, 128, 1024], P(None, None, 'tm')
All inputs are finite; a program needn't handle non-finite values.
Results may differ from a plain program's by a relative error of at most 0.0003.
Values sent between devices are 32-bit elements; how exact they have to be, the bound alone decides.
No kernel may reach another device: no remote copies, remote signals or barrier semaphores. Data moves between devices by JAX's collectives and lax.ppermute only.
A program may use at most 64 MiB of HBM per device.

v0:
```python
import functools

import jax
import jax.numpy as jnp
from jax import lax
from jax.experimental import pallas as pl
from jax.experimental.pallas import tpu as pltpu
from jax.sharding import Mesh
from jax.sharding import PartitionSpec as P


GRID = (8, 8, 2)
CORE = "core_of_chip"
YZ = ("mom_0", "mom_1")
VMEM_LIMIT = 32 << 20
SUB = 4
LANES = 128


def near(value):
    return pltpu.with_memory_space_constraint(value, pltpu.VMEM)


def far(value):
    return pltpu.with_memory_space_constraint(value, pltpu.HBM)


def near_out(shape, dtype=jnp.float32):
    return pltpu.VMEM(shape, dtype)


def far_out(shape, dtype=jnp.float32):
    return pltpu.HBM(shape, dtype)


def call(kernel, inputs, outputs, scratch=()):
    vmem = pl.BlockSpec(memory_space=pltpu.VMEM)
    return pl.pallas_call(
        kernel,
        out_shape=tuple(outputs),
        in_specs=[vmem] * len(inputs),
        out_specs=(vmem,) * len(outputs),
        scratch_shapes=scratch,
        compiler_params=pltpu.CompilerParams(vmem_limit_bytes=VMEM_LIMIT),
    )(*[near(value) for value in inputs])


def halves_of(value):
    high = value.astype(jnp.bfloat16)
    return high, (value - high.astype(jnp.float32)).astype(jnp.bfloat16)


def packed(real, imag):
    top = lax.broadcasted_iota(jnp.int32, real.shape, 0) < SUB
    return jnp.where(top, real, jnp.roll(imag, SUB, 0)), jnp.where(top, jnp.roll(real, SUB, 0), imag)


def store_packed(store, real, imag):
    rows, cols = real.shape
    wide = cols // LANES
    for pair in range(rows // 8):
        for h in range(wide):
            window = (slice(8 * pair, 8 * pair + 8), slice(LANES * h, LANES * h + LANES))
            first, second = packed(real[window], imag[window])
            store((2 * pair) * wide + h, first)
            store((2 * pair + 1) * wide + h, second)


def pack_kernel(sigma_ref, out_ref):
    copies, pieces = out_ref.shape[:2]
    comps, rows = sigma_ref.shape[0], sigma_ref.shape[1] // 2
    mine = pl.ds(pl.multiple_of(lax.axis_index(CORE) * rows, 8), rows)

    for orbital in range(comps // 2):

        def store(index, tile, orbital=orbital):
            for copy in range(copies):
                out_ref[copy, orbital * (pieces // (comps // 2)) + index] = tile

        store_packed(store, sigma_ref[2 * orbital, mine, :], sigma_ref[2 * orbital + 1, mine, :])


def pack(sigma, copies):
    comps, rows, cols = sigma.shape
    pieces = comps // 2 * (rows // 2) * cols // (SUB * LANES)
    return call(pack_kernel, [sigma], [far_out((copies, pieces, 8, LANES))])[0]


def split_kernel(history_ref, high_ref, low_ref, last_ref):
    _, rows, cols = history_ref.shape
    keep_rows = last_ref.shape[1]
    col_ids = lax.axis_index("tm") * cols + lax.broadcasted_iota(jnp.int32, (rows, cols), 1)
    keep = col_ids <= lax.broadcasted_iota(jnp.int32, (rows, cols), 0)
    high, low = halves_of(jnp.where(keep, history_ref[0], 0.0))
    high_ref[0] = high
    low_ref[0] = low
    start = rows - 2 * keep_rows + lax.axis_index(CORE) * keep_rows
    row_ids = start + lax.broadcasted_iota(jnp.int32, (keep_rows, cols), 0)
    mine = pl.ds(pl.multiple_of(start, 8), keep_rows)
    last_ref[0] = jnp.where(col_ids[:keep_rows] <= row_ids, history_ref[0, mine, :], 0.0)


def split(history, keep_rows):
    comps, rows, cols = history.shape
    whole = pl.BlockSpec((1, rows, cols), lambda i: (i, 0, 0))
    return pl.pallas_call(
        split_kernel,
        out_shape=(
            far_out(history.shape, jnp.bfloat16),
            far_out(history.shape, jnp.bfloat16),
            far_out((comps, keep_rows, cols)),
        ),
        grid=(comps,),
        in_specs=[whole],
        out_specs=(whole, whole, pl.BlockSpec((1, keep_rows, cols), lambda i: (i, 0, 0))),
        compiler_params=pltpu.CompilerParams(vmem_limit_bytes=VMEM_LIMIT),
        name="split",
    )(far(history))


def block_kernel(block, windows, stacked, step_size, *refs):
    count = 4 + (1 if stacked else 2) + 2 * windows
    factor_ref, sigma_ref, sources = refs[0], refs[1], refs[2 : 2 + count]
    outs, buffers, arrived = refs[2 + count : -(count + 3)], refs[-(count + 3) : -3], refs[-3]
    piece_ref, outs = outs[-1], outs[:-1]
    sigma_scratch, joined = refs[-2:]
    highs, lows = buffers[:2], buffers[2:4]
    previous = (buffers[4].at[0], buffers[4].at[1]) if stacked else buffers[4:6]
    mine_refs, theirs_refs = buffers[-2 * windows : count - windows], buffers[count - windows :]
    comps, rows, cols = previous[0].shape
    orbitals = comps // 2
    known_rows = highs[0].shape[1]
    used = known_rows + windows * 2 * rows
    wide = cols // LANES
    per_orbital = piece_ref.shape[0] // orbitals

    def part_of(ref, orbital):
        span = pl.ds(2 * orbital, 2)
        return ref.at[span] if len(ref.shape) == 3 else ref.at[:, span]

    copies = [
        [
            pltpu.make_async_copy(part_of(source, o), part_of(buffer, o), arrived.at[o, i])
            for i, (source, buffer) in enumerate(zip(sources, buffers, strict=True))
        ]
        for o in range(orbitals)
    ]
    for of_orbital in copies:
        for copy in of_orbital:
            copy.start()
    core = lax.axis_index(CORE)
    mine_at = pl.ds(pl.multiple_of(core * rows, 8), rows)
    theirs_at = pl.ds(pl.multiple_of((1 - core) * rows, 8), rows)
    top = lax.broadcasted_iota(jnp.int32, (8, LANES), 0) < SUB
    row_ids = known_rows + block * 2 * rows + core * rows + lax.broadcasted_iota(jnp.int32, (rows, cols), 0)
    keep = lax.axis_index("tm") * cols + lax.broadcasted_iota(jnp.int32, (rows, cols), 1) <= row_ids

    def product(span, high, low):
        both = jnp.dot(sigma_scratch[:, span], high, preferred_element_type=jnp.float32)
        rest = jnp.dot(sigma_scratch[: 2 * rows, span], low, preferred_element_type=jnp.float32)
        return both[: 2 * rows] + (both[2 * rows :] + rest)

    for orbital in range(orbitals):
        base = orbital * per_orbital
        for tile in range(pl.cdiv(used, LANES)):
            shard, h = tile // wide, tile % wide
            reals, imags = [], []
            for pair in range(rows // 8):
                first = sigma_ref[shard, base + (2 * pair) * wide + h]
                second = sigma_ref[shard, base + (2 * pair + 1) * wide + h]
                reals.append(jnp.where(top, first, jnp.roll(second, SUB, 0)))
                imags.append(jnp.where(top, jnp.roll(first, SUB, 0), second))
            high, low = halves_of(jnp.concatenate(reals + imags, 0))
            lanes = slice(LANES * tile, LANES * tile + LANES)
            sigma_scratch[: 2 * rows, lanes] = high
            sigma_scratch[2 * rows :, lanes] = low
        for copy in copies[orbital]:
            copy.wait()

        totals = None
        for momentum in range(2):
            products = []
            for part in range(2 * orbital, 2 * orbital + 2):
                total = product(slice(0, known_rows), highs[momentum][part], lows[momentum][part])
                for window in range(windows):
                    joined[mine_at, :] = mine_refs[window][momentum, part]
                    joined[theirs_at, :] = theirs_refs[window][1 - momentum, part]
                    start = known_rows + window * 2 * rows
                    total = total + product(slice(start, start + 2 * rows), *halves_of(joined[...]))
                products.append(total)
            by_real, by_imag = products
            x_re = previous[momentum][2 * orbital] + step_size * (by_real[:rows] - by_imag[rows:])
            x_im = previous[momentum][2 * orbital + 1] + step_size * (by_imag[:rows] + by_real[rows:])
            p_re = factor_ref[block, orbital, :, momentum : momentum + 1]
            p_im = factor_ref[block, orbital, :, 2 + momentum : 3 + momentum]
            real = jnp.where(keep, p_re * x_re - p_im * x_im, 0.0)
            imag = jnp.where(keep, p_re * x_im + p_im * x_re, 0.0)
            out = outs[0].at[momentum] if len(outs) == 1 else outs[momentum]
            out[2 * orbital] = real
            out[2 * orbital + 1] = imag
            totals = (real, imag) if totals is None else (totals[0] + real, totals[1] + imag)

        def store(index, tile, base=base):
            piece_ref[base + index] = tile

        store_packed(store, *totals)


def advance(block, last, step_size, sigma, factors, highs, lows, previous, mine, theirs):
    comps, known_rows, cols = highs[0].shape
    rows = factors.shape[2]
    used = pl.cdiv(known_rows + len(mine) * 2 * rows, LANES) * LANES
    sources = [*highs, *lows, *previous, *mine, *theirs]
    greens = [far_out((comps, rows, cols))] * 2 if last else [far_out((2, comps, rows, cols))]
    vmem = pl.BlockSpec(memory_space=pltpu.VMEM)
    *greens, pieces = pl.pallas_call(
        functools.partial(block_kernel, block, len(mine), len(previous) == 1, step_size),
        out_shape=(*greens, near_out((sigma.shape[1], 8, LANES))),
        in_specs=[vmem, vmem] + [pl.BlockSpec(memory_space=pl.ANY)] * len(sources),
        out_specs=(vmem,) * (len(greens) + 1),
        scratch_shapes=[
            *[pltpu.VMEM(source.shape, source.dtype) for source in sources],
            pltpu.SemaphoreType.DMA((comps // 2, len(sources))),
            pltpu.VMEM((4 * rows, used), jnp.bfloat16),
            pltpu.VMEM((2 * rows, cols), jnp.float32),
        ],
        compiler_params=pltpu.CompilerParams(vmem_limit_bytes=VMEM_LIMIT),
    )(factors, near(sigma), *[far(source) for source in sources])
    return greens, pieces


def cube_kernel(norm_factor, parts_ref, out_ref):
    sums = [parts_ref[i] for i in range(4)]
    for i in range(4, parts_ref.shape[0]):
        sums[i % 4] = sums[i % 4] + parts_ref[i]
    local = ((sums[0] + sums[1]) + (sums[2] + sums[3])) * norm_factor
    paired = jnp.roll(local, SUB, 0)
    value = 0.1 * (local * local * local - 3.0 * local * paired * paired)
    top = lax.broadcasted_iota(jnp.int32, local.shape, 0) < SUB
    value = jnp.where(top, value, -value)
    for i in range(out_ref.shape[0]):
        out_ref[i] = value


def cube(parts, norm_factor):
    kernel = functools.partial(cube_kernel, norm_factor)
    return call(kernel, [parts], [near_out(parts.shape)])[0]


def copies_kernel(value_ref, out_ref):
    for i in range(out_ref.shape[0]):
        out_ref[i] = value_ref[...]


def copies_of(value, count):
    return call(copies_kernel, [value], [far_out((count, *value.shape))])[0]


def green_kernel(mine_ref, theirs_ref, out_ref):
    rows = mine_ref.shape[1]
    core = lax.axis_index(CORE)
    out_ref[:, pl.ds(pl.multiple_of(core * rows, 8), rows), :] = mine_ref[...]
    out_ref[:, pl.ds(pl.multiple_of((1 - core) * rows, 8), rows), :] = theirs_ref[...]


def sigma_kernel(mine_ref, theirs_ref, out_ref):
    comps, rows, cols = out_ref.shape
    rows = rows // 2
    wide = cols // LANES
    core = lax.axis_index(CORE)
    top = lax.broadcasted_iota(jnp.int32, (8, LANES), 0) < SUB
    per_orbital = mine_ref.shape[0] // (comps // 2)
    for start, ref in ((core * rows, mine_ref), ((1 - core) * rows, theirs_ref)):
        for orbital in range(comps // 2):
            for pair in range(rows // 8):
                at = pl.ds(pl.multiple_of(start + 8 * pair, 8), 8)
                for h in range(wide):
                    first = ref[orbital * per_orbital + (2 * pair) * wide + h]
                    second = ref[orbital * per_orbital + (2 * pair + 1) * wide + h]
                    lanes = slice(LANES * h, LANES * h + LANES)
                    out_ref[2 * orbital, at, lanes] = jnp.where(top, first, jnp.roll(second, SUB, 0))
                    out_ref[2 * orbital + 1, at, lanes] = jnp.where(top, jnp.roll(first, SUB, 0), second)


def body(history, sigma_first, propagator):
    history, propagator = history[:, 0], propagator[:, 0]
    comps, _, cols = history.shape
    rows_block = sigma_first.shape[1]
    blocks = propagator.shape[1] // rows_block
    rows = rows_block // 2
    shards = lax.axis_size("tm")
    step_size = 1.0 / float(cols * shards) ** 0.5
    norm_factor = 1.0 / float(lax.axis_size(YZ) * lax.axis_size(CORE)) ** 0.5
    core = lax.axis_index(CORE)

    def swapped(value):
        return lax.ppermute(value, CORE, [(0, 1), (1, 0)])

    packed_first = pack(sigma_first, shards)
    sigma = lax.all_to_all(packed_first, "tm", 0, 0, tiled=True)
    their_history = swapped(history)
    their_propagator = swapped(propagator)
    own = split(history, rows)
    other = split(their_history, rows)
    highs, lows, greens = (own[0], other[0]), (own[1], other[1]), (own[2], other[2])
    factors = jnp.stack([propagator, their_propagator]).reshape(2, comps // 2, 2, blocks, 2, rows)
    factors = lax.dynamic_index_in_dim(factors, core, 4, keepdims=False)
    factors = factors.transpose(3, 1, 4, 2, 0).reshape(blocks, comps // 2, rows, 4)
    mine, theirs = [], []
    for block in range(blocks):
        last = block + 1 == blocks
        greens, pieces = advance(block, last, step_size, sigma, factors, highs, lows, greens, mine, theirs)
        parts = lax.all_to_all(pieces, YZ, 0, 0, tiled=True)
        sigma = lax.all_to_all(cube(parts, norm_factor), YZ, 0, 0, tiled=True)
        if not last:
            mine.append(greens[0])
            theirs.append(swapped(greens[0]))
            sigma = lax.all_to_all(copies_of(sigma, shards), "tm", 0, 0, tiled=True)
    whole = [far_out((comps, rows_block, cols))]
    green_last = call(green_kernel, [greens[0], swapped(greens[1])], whole)[0]
    sigma_next = call(sigma_kernel, [sigma, swapped(sigma)], whole)[0]
    return green_last[:, None], sigma_next


def solution(mesh):
    torus = Mesh(mesh.devices.reshape(*GRID, mesh.shape["tm"]), (*YZ, CORE, "tm"))
    moms = (*YZ, CORE)
    return jax.shard_map(
        body,
        mesh=torus,
        in_specs=(P(None, moms, None, "tm"), P(None, None, "tm"), P(None, moms, None)),
        out_specs=(P(None, moms, None, "tm"), P(None, None, "tm")),
        check_vma=False,
    )
```

profile of v0, /device:TPU:1, one launch (start us, length us, event | category | flops | bytes accessed | tf_op | source)
XLA Modules:
  0.0 203.4 jit_solution(14097104426396164164)
XLA Ops:
  0.6 8.8 %collective-permute-start.1 = (f32[4,640,256]{2,1,0:T(8,128)}, f32[4,640,256]{2,1,0:T(8,128)}, u32[]{:S(2)}, u32[]{:S(2)}) collective-permute-start(f32[4,640,256]{2,1,0:T(8,128)} %bitcast.12), channel_id=1, source_target_pairs={{0,4},{4,0},{1,5},{5,1},{2,6},{6,2},{3,7},{7,3},{8,12},{12,8},{9,1... | collective-permute-start | bytes 7864328 | tf_op jit(solution)/shard_map/ppermute | solution.py:297
  9.4 0.0 copy-start
  9.4 1.0 copy-done
  10.4 1.1 shard_map.50
  11.6 3.6 %all-to-all-start = ((f32[4,64,8,128]{3,2,1,0:T(8,128)}), f32[4,64,8,128]{3,2,1,0:T(8,128)S(1)}, u32[]{:S(2)}, u32[]{:S(2)}) async-start(f32[4,64,8,128]{3,2,1,0:T(8,128)} %shard_map.50), calls=%async_computation | async-start | bytes 2097152 | tf_op jit(solution)/shard_map/all_to_all | solution.py:300
  15.2 0.0 copy-done.6
  15.2 1.9 collective-permute-start
  17.2 4.2 %split.2 = (bf16[4,640,256]{2,1,0:T(8,128)(2,1)}, bf16[4,640,256]{2,1,0:T(8,128)(2,1)}, f32[4,64,256]{2,1,0:T(8,128)}) custom-call(f32[4,640,256]{2,1,0:T(8,128)} %bitcast.13), custom_call_target="tpu_custom_call" | custom-call | tf_op jit(solution)/shard_map/split/pallas_call | solution.py:106
  21.4 0.1 stack.8
  21.5 0.0 collective-permute-done
  21.5 0.1 stack.9
  21.6 0.1 copy.10.refs_0_
  21.7 0.0 collective-permute-done.1.history_ref
  21.8 4.3 %split.3 = (bf16[4,640,256]{2,1,0:T(8,128)(2,1)}, bf16[4,640,256]{2,1,0:T(8,128)(2,1)}, f32[4,64,256]{2,1,0:T(8,128)}) custom-call(f32[4,640,256]{2,1,0:T(8,128)} %collective-permute-done.1.history_ref), custom_call_target="tpu_custom_call" | custom-call | tf_op jit(solution)/shard_map/split/pallas_call | solution.py:106
  26.1 4.3 %all-to-all-done.refs_1_ = f32[4,64,8,128]{3,2,1,0:T(8,128)S(1)} async-done(((f32[4,64,8,128]{3,2,1,0:T(8,128)}), f32[4,64,8,128]{3,2,1,0:T(8,128)S(1)}, u32[]{:S(2)}, u32[]{:S(2)}) %all-to-all-start) | async-done | bytes 1048608 | tf_op jit(solution)/shard_map/all_to_all | solution.py:300
  30.4 4.3 %shard_map.51 = (f32[2,4,64,256]{3,2,1,0:T(8,128)}, f32[64,8,128]{2,1,0:T(8,128)S(1)}) custom-call(f32[3,2,64,4]{3,2,1,0:T(8,128)S(1)} %copy.10.refs_0_, f32[4,64,8,128]{3,2,1,0:T(8,128)S(1)} %all-to-all-done.refs_1_, bf16[4,640,256]{2,1,0:T(8,128)(2,1)} %get-tuple-element.15.refs_2_, bf16[4,640,256]{2,1,0:T(8,128)(2,1)} %get-tuple-element.16.refs_3_, ...), custom_call_target="tpu_custom_call" | custom-call | tf_op jit(solution)/shard_map/pallas_call | solution.py:216
  34.7 23.4 %all_to_all.45.parts_ref = f32[64,8,128]{2,1,0:T(8,128)S(1)} all-to-all(f32[64,8,128]{2,1,0:T(8,128)S(1)} %get-tuple-element.21), channel_id=1, replica_groups=mesh['mom_0'=8,'mom_1'=8,'core_of_chip'=2,'tm'=4] {'mom_0','mom_1'}, dimensions={0} | all-to-all | bytes 524288 | tf_op jit(solution)/shard_map/all_to_all | solution.py:313
  58.2 18.4 %all_to_all.46.value_ref = f32[64,8,128]{2,1,0:T(8,128)S(1)} all-to-all(f32[64,8,128]{2,1,0:T(8,128)S(1)} %shard_map.52), channel_id=1, replica_groups=mesh['mom_0'=8,'mom_1'=8,'core_of_chip'=2,'tm'=4] {'mom_0','mom_1'}, dimensions={0} | all-to-all | bytes 524288 | tf_op jit(solution)/shard_map/all_to_all | solution.py:314
  76.6 1.1 shard_map.53
  77.6 3.6 %all-to-all-start.3 = ((f32[4,64,8,128]{3,2,1,0:T(8,128)}), f32[4,64,8,128]{3,2,1,0:T(8,128)S(1)}, u32[]{:S(2)}, u32[]{:S(2)}) async-start(f32[4,64,8,128]{3,2,1,0:T(8,128)} %shard_map.53), calls=%async_computation.3 | async-start | bytes 2097152 | tf_op jit(solution)/shard_map/all_to_all | solution.py:318
  81.3 0.0 copy-done.2
  81.3 5.4 %collective-permute-start.2 = (f32[2,4,64,256]{3,2,1,0:T(8,128)S(1)}, f32[2,4,64,256]{3,2,1,0:T(8,128)S(1)}, u32[]{:S(2)}, u32[]{:S(2)}) collective-permute-start(f32[2,4,64,256]{3,2,1,0:T(8,128)S(1)} %copy-done.2), channel_id=1, source_target_pairs={{0,4},{4,0},{1,5},{5,1},{2,6},{6,2},{3,7},{7,3},{8,12},{12,8},{9,1... | collective-permute-start | bytes 1572872 | tf_op jit(solution)/shard_map/ppermute | solution.py:297
  86.7 1.5 collective-permute-done.2.refs_8_.refs_9_
  88.2 4.5 %all-to-all-done.3.refs_1_ = f32[4,64,8,128]{3,2,1,0:T(8,128)S(1)} async-done(((f32[4,64,8,128]{3,2,1,0:T(8,128)}), f32[4,64,8,128]{3,2,1,0:T(8,128)S(1)}, u32[]{:S(2)}, u32[]{:S(2)}) %all-to-all-start.3) | async-done | bytes 1048608 | tf_op jit(solution)/shard_map/all_to_all | solution.py:318
  92.7 0.0 copy-done.4
  92.7 5.1 %shard_map.54 = (f32[2,4,64,256]{3,2,1,0:T(8,128)}, f32[64,8,128]{2,1,0:T(8,128)S(1)}) custom-call(f32[3,2,64,4]{3,2,1,0:T(8,128)S(1)} %copy.10.refs_0_, f32[4,64,8,128]{3,2,1,0:T(8,128)S(1)} %all-to-all-done.3.refs_1_, bf16[4,640,256]{2,1,0:T(8,128)(2,1)} %get-tuple-element.15.refs_2_, bf16[4,640,256]{2,1,0:T(8,128)(2,1)} %get-tuple-element.16.refs_3_, ...), custom_call_target="tpu_custom_call" | custom-call | tf_op jit(solution)/shard_map/pallas_call | solution.py:216
  97.8 21.2 %all_to_all.47.parts_ref = f32[64,8,128]{2,1,0:T(8,128)S(1)} all-to-all(f32[64,8,128]{2,1,0:T(8,128)S(1)} %get-tuple-element.23), channel_id=1, replica_groups=mesh['mom_0'=8,'mom_1'=8,'core_of_chip'=2,'tm'=4] {'mom_0','mom_1'}, dimensions={0} | all-to-all | bytes 524288 | tf_op jit(solution)/shard_map/all_to_all | solution.py:313
  119.0 17.0 %all_to_all.48.value_ref = f32[64,8,128]{2,1,0:T(8,128)S(1)} all-to-all(f32[64,8,128]{2,1,0:T(8,128)S(1)} %shard_map.55), channel_id=1, replica_groups=mesh['mom_0'=8,'mom_1'=8,'core_of_chip'=2,'tm'=4] {'mom_0','mom_1'}, dimensions={0} | all-to-all | bytes 524288 | tf_op jit(solution)/shard_map/all_to_all | solution.py:314
  136.0 1.1 shard_map.56
  137.1 3.6 %all-to-all-start.6 = ((f32[4,64,8,128]{3,2,1,0:T(8,128)}), f32[4,64,8,128]{3,2,1,0:T(8,128)S(1)}, u32[]{:S(2)}, u32[]{:S(2)}) async-start(f32[4,64,8,128]{3,2,1,0:T(8,128)} %shard_map.56), calls=%async_computation.6 | async-start | bytes 2097152 | tf_op jit(solution)/shard_map/all_to_all | solution.py:318
  140.7 0.0 copy-done.3
  140.7 6.0 %collective-permute-start.3 = (f32[2,4,64,256]{3,2,1,0:T(8,128)S(1)}, f32[2,4,64,256]{3,2,1,0:T(8,128)S(1)}, u32[]{:S(2)}, u32[]{:S(2)}) collective-permute-start(f32[2,4,64,256]{3,2,1,0:T(8,128)S(1)} %copy-done.3), channel_id=1, source_target_pairs={{0,4},{4,0},{1,5},{5,1},{2,6},{6,2},{3,7},{7,3},{8,12},{12,8},{9,1... | collective-permute-start | bytes 1572872 | tf_op jit(solution)/shard_map/ppermute | solution.py:297
  146.8 1.5 collective-permute-done.3.refs_10_
  148.3 3.2 %all-to-all-done.6.refs_1_ = f32[4,64,8,128]{3,2,1,0:T(8,128)S(1)} async-done(((f32[4,64,8,128]{3,2,1,0:T(8,128)}), f32[4,64,8,128]{3,2,1,0:T(8,128)S(1)}, u32[]{:S(2)}, u32[]{:S(2)}) %all-to-all-start.6) | async-done | bytes 1048608 | tf_op jit(solution)/shard_map/all_to_all | solution.py:318
  151.5 5.8 %shard_map.57 = (f32[4,64,256]{2,1,0:T(8,128)}, f32[4,64,256]{2,1,0:T(8,128)}, f32[64,8,128]{2,1,0:T(8,128)S(1)}) custom-call(f32[3,2,64,4]{3,2,1,0:T(8,128)S(1)} %copy.10.refs_0_, f32[4,64,8,128]{3,2,1,0:T(8,128)S(1)} %all-to-all-done.6.refs_1_, bf16[4,640,256]{2,1,0:T(8,128)(2,1)} %get-tuple-element.15.refs_2_, ...), custom_call_target="tpu_custom_call" | custom-call | tf_op jit(solution)/shard_map/pallas_call | solution.py:216
  157.3 0.0 copy-start.7
  157.3 0.0 copy-start.1
  157.3 17.1 %all_to_all.49.parts_ref = f32[64,8,128]{2,1,0:T(8,128)S(1)} all-to-all(f32[64,8,128]{2,1,0:T(8,128)S(1)} %get-tuple-element.27), channel_id=1, replica_groups=mesh['mom_0'=8,'mom_1'=8,'core_of_chip'=2,'tm'=4] {'mom_0','mom_1'}, dimensions={0} | all-to-all | bytes 524288 | tf_op jit(solution)/shard_map/all_to_all | solution.py:313
  174.5 0.7 shard_map.59
  175.2 4.6 %all-to-all-start.8 = ((f32[64,8,128]{2,1,0:T(8,128)}), f32[64,8,128]{2,1,0:T(8,128)S(1)}, u32[]{:S(2)}, u32[]{:S(2)}) async-start(f32[64,8,128]{2,1,0:T(8,128)} %shard_map.59), calls=%async_computation.8 | async-start | bytes 524288 | tf_op jit(solution)/shard_map/all_to_all | solution.py:314
  179.8 7.9 %collective-permute-start.4 = (f32[4,64,256]{2,1,0:T(8,128)S(1)}, f32[4,64,256]{2,1,0:T(8,128)S(1)}, u32[]{:S(2)}, u32[]{:S(2)}) collective-permute-start(f32[4,64,256]{2,1,0:T(8,128)S(1)} %copy-done.7), channel_id=1, source_target_pairs={{0,4},{4,0},{1,5},{5,1},{2,6},{6,2},{3,7},{7,3},{8,12},{12,8},{9,1... | collective-permute-start | bytes 786440 | tf_op jit(solution)/shard_map/ppermute | solution.py:297
  187.7 4.7 %all-to-all-done.8.mine_ref = f32[64,8,128]{2,1,0:T(8,128)S(1)} async-done(((f32[64,8,128]{2,1,0:T(8,128)}), f32[64,8,128]{2,1,0:T(8,128)S(1)}, u32[]{:S(2)}, u32[]{:S(2)}) %all-to-all-start.8) | async-done | bytes 262176 | tf_op jit(solution)/shard_map/all_to_all | solution.py:314
  192.4 8.9 %collective-permute-start.5 = (f32[64,8,128]{2,1,0:T(8,128)S(1)}, f32[64,8,128]{2,1,0:T(8,128)S(1)}, u32[]{:S(2)}, u32[]{:S(2)}) collective-permute-start(f32[64,8,128]{2,1,0:T(8,128)S(1)} %all-to-all-done.8.mine_ref), channel_id=1, source_target_pairs={{0,4},{4,0},{1,5},{5,1},{2,6},{6,2},{3,7},{7,3},{8,12},{12,8},{9,1... | collective-permute-start | bytes 786440 | tf_op jit(solution)/shard_map/ppermute | solution.py:297
  201.4 0.0 collective-permute-done.4.theirs_ref
  201.4 0.0 copy-done.1
  201.4 0.8 shard_map.58
  202.2 0.3 collective-permute-done.5.theirs_ref
  202.5 0.8 shard_map.60
  (13 shorter events, 0.2 us)
Async XLA Ops:
  0.6 21.1 %collective-permute-start.1 = (f32[4,640,256]{2,1,0:T(8,128)}, f32[4,640,256]{2,1,0:T(8,128)}, u32[]{:S(2)}, u32[]{:S(2)}) collective-permute-start(f32[4,640,256]{2,1,0:T(8,128)} %bitcast.12), channel_id=1, source_target_pairs={{0,4},{4,0},{1,5},{5,1},{2,6},{6,2},{3,7},{7,3},{8,12},{12,8},{9,1... | collective-permute-start | bytes 7864328 | tf_op jit(solution)/shard_map/ppermute | solution.py:297
  9.4 1.0 copy-start
  11.6 3.7 %copy-start.6 = (f32[4,1,384]{2,1,0:T(1,128)S(1)}, f32[4,1,384]{2,1,0:T(1,128)}, u32[]{:S(2)}) copy-start(f32[4,1,384]{2,1,0:T(1,128)} %param.5) | copy-start | bytes 18436
  11.6 18.8 %all-to-all-start = ((f32[4,64,8,128]{3,2,1,0:T(8,128)}), f32[4,64,8,128]{3,2,1,0:T(8,128)S(1)}, u32[]{:S(2)}, u32[]{:S(2)}) async-start(f32[4,64,8,128]{3,2,1,0:T(8,128)} %shard_map.50), calls=%async_computation | async-start | bytes 2097152 | tf_op jit(solution)/shard_map/all_to_all | solution.py:300
  15.2 6.3 %collective-permute-start = (f32[4,384]{1,0:T(4,128)S(1)}, f32[4,384]{1,0:T(4,128)S(1)}, u32[]{:S(2)}, u32[]{:S(2)}) collective-permute-start(f32[4,384]{1,0:T(4,128)S(1)} %bitcast.16), channel_id=1, source_target_pairs={{0,4},{4,0},{1,5},{5,1},{2,6},{6,2},{3,7},{7,3},{8,12},{12,8},{9,1... | collective-permute-start | bytes 18440 | tf_op jit(solution)/shard_map/ppermute | solution.py:297
  77.6 3.7 %copy-start.2 = (f32[2,4,64,256]{3,2,1,0:T(8,128)S(1)}, f32[2,4,64,256]{3,2,1,0:T(8,128)}, u32[]{:S(2)}) copy-start(f32[2,4,64,256]{3,2,1,0:T(8,128)} %get-tuple-element.22.refs_6_.refs_7_) | copy-start | bytes 1572868
  77.6 15.0 %all-to-all-start.3 = ((f32[4,64,8,128]{3,2,1,0:T(8,128)}), f32[4,64,8,128]{3,2,1,0:T(8,128)S(1)}, u32[]{:S(2)}, u32[]{:S(2)}) async-start(f32[4,64,8,128]{3,2,1,0:T(8,128)} %shard_map.53), calls=%async_computation.3 | async-start | bytes 2097152 | tf_op jit(solution)/shard_map/all_to_all | solution.py:318
  81.3 6.9 %collective-permute-start.2 = (f32[2,4,64,256]{3,2,1,0:T(8,128)S(1)}, f32[2,4,64,256]{3,2,1,0:T(8,128)S(1)}, u32[]{:S(2)}, u32[]{:S(2)}) collective-permute-start(f32[2,4,64,256]{3,2,1,0:T(8,128)S(1)} %copy-done.2), channel_id=1, source_target_pairs={{0,4},{4,0},{1,5},{5,1},{2,6},{6,2},{3,7},{7,3},{8,12},{12,8},{9,1... | collective-permute-start | bytes 1572872 | tf_op jit(solution)/shard_map/ppermute | solution.py:297
  88.2 4.5 %copy-start.4 = (f32[2,4,64,256]{3,2,1,0:T(8,128)}, f32[2,4,64,256]{3,2,1,0:T(8,128)S(1)}, u32[]{:S(2)}) copy-start(f32[2,4,64,256]{3,2,1,0:T(8,128)S(1)} %collective-permute-done.2.refs_8_.refs_9_) | copy-start | bytes 1572868
  137.1 3.7 %copy-start.3 = (f32[2,4,64,256]{3,2,1,0:T(8,128)S(1)}, f32[2,4,64,256]{3,2,1,0:T(8,128)}, u32[]{:S(2)}) copy-start(f32[2,4,64,256]{3,2,1,0:T(8,128)} %get-tuple-element.24.refs_6_.refs_8_) | copy-start | bytes 1572868
  137.1 14.4 %all-to-all-start.6 = ((f32[4,64,8,128]{3,2,1,0:T(8,128)}), f32[4,64,8,128]{3,2,1,0:T(8,128)S(1)}, u32[]{:S(2)}, u32[]{:S(2)}) async-start(f32[4,64,8,128]{3,2,1,0:T(8,128)} %shard_map.56), calls=%async_computation.6 | async-start | bytes 2097152 | tf_op jit(solution)/shard_map/all_to_all | solution.py:318
  140.7 7.5 %collective-permute-start.3 = (f32[2,4,64,256]{3,2,1,0:T(8,128)S(1)}, f32[2,4,64,256]{3,2,1,0:T(8,128)S(1)}, u32[]{:S(2)}, u32[]{:S(2)}) collective-permute-start(f32[2,4,64,256]{3,2,1,0:T(8,128)S(1)} %copy-done.3), channel_id=1, source_target_pairs={{0,4},{4,0},{1,5},{5,1},{2,6},{6,2},{3,7},{7,3},{8,12},{12,8},{9,1... | collective-permute-start | bytes 1572872 | tf_op jit(solution)/shard_map/ppermute | solution.py:297
  148.3 3.2 %copy-start.5 = (f32[2,4,64,256]{3,2,1,0:T(8,128)}, f32[2,4,64,256]{3,2,1,0:T(8,128)S(1)}, u32[]{:S(2)}) copy-start(f32[2,4,64,256]{3,2,1,0:T(8,128)S(1)} %collective-permute-done.3.refs_10_) | copy-start | bytes 1572868
  157.3 22.5 %copy-start.7 = (f32[4,64,256]{2,1,0:T(8,128)S(1)}, f32[4,64,256]{2,1,0:T(8,128)}, u32[]{:S(2)}) copy-start(f32[4,64,256]{2,1,0:T(8,128)} %get-tuple-element.26) | copy-start | bytes 786436
  157.3 44.1 %copy-start.1 = (f32[4,64,256]{2,1,0:T(8,128)S(1)}, f32[4,64,256]{2,1,0:T(8,128)}, u32[]{:S(2)}) copy-start(f32[4,64,256]{2,1,0:T(8,128)} %get-tuple-element.25.mine_ref) | copy-start | bytes 786436
  175.2 17.2 %all-to-all-start.8 = ((f32[64,8,128]{2,1,0:T(8,128)}), f32[64,8,128]{2,1,0:T(8,128)S(1)}, u32[]{:S(2)}, u32[]{:S(2)}) async-start(f32[64,8,128]{2,1,0:T(8,128)} %shard_map.59), calls=%async_computation.8 | async-start | bytes 524288 | tf_op jit(solution)/shard_map/all_to_all | solution.py:314
  179.8 21.5 %collective-permute-start.4 = (f32[4,64,256]{2,1,0:T(8,128)S(1)}, f32[4,64,256]{2,1,0:T(8,128)S(1)}, u32[]{:S(2)}, u32[]{:S(2)}) collective-permute-start(f32[4,64,256]{2,1,0:T(8,128)S(1)} %copy-done.7), channel_id=1, source_target_pairs={{0,4},{4,0},{1,5},{5,1},{2,6},{6,2},{3,7},{7,3},{8,12},{12,8},{9,1... | collective-permute-start | bytes 786440 | tf_op jit(solution)/shard_map/ppermute | solution.py:297
  192.4 10.1 %collective-permute-start.5 = (f32[64,8,128]{2,1,0:T(8,128)S(1)}, f32[64,8,128]{2,1,0:T(8,128)S(1)}, u32[]{:S(2)}, u32[]{:S(2)}) collective-permute-start(f32[64,8,128]{2,1,0:T(8,128)S(1)} %all-to-all-done.8.mine_ref), channel_id=1, source_target_pairs={{0,4},{4,0},{1,5},{5,1},{2,6},{6,2},{3,7},{7,3},{8,12},{12,8},{9,1... | collective-permute-start | bytes 786440 | tf_op jit(solution)/shard_map/ppermute | solution.py:297
where the time goes:
time: 204 us; the launch traced here: 203 us
  blocking collectives  97.2 us (48%)
  starting transfers between devices  54.5 us (27%)
  Pallas kernels  29.5 us (14%)
  waiting for transfers between devices  20 us (10%)
    all_to_all x3, blocking collectives, body(): parts = lax.all_to_all(pieces, YZ, 0, 0, tiled=True)  61.7 us
    ppermute x6, starting transfers between devices, swapped(): return lax.ppermute(value, CORE, [(0, 1), (1, 0)])  38.9 us
    all_to_all x2, blocking collectives, body(): sigma = lax.all_to_all(cube(parts, norm_factor), YZ, 0, 0, tiled=True)  35.4 us
    pallas_call x3, Pallas kernels, advance(): pl.pallas_call(functools.partial(block_kernel, block, len(mine), len(prev...  15.2 us
    pallas_call x2, Pallas kernels, split(): pl.pallas_call(split_kernel, out_shape=(far_out(history.shape, jnp.bfloat...  8.5 us
    all_to_all x2, waiting for transfers between devices, body(): sigma = lax.all_to_all(copies_of(sigma, shards), 'tm', 0, 0, tiled=True)  7.67 us
    all_to_all x2, starting transfers between devices, body(): sigma = lax.all_to_all(copies_of(sigma, shards), 'tm', 0, 0, tiled=True)  7.29 us
    pallas_call x8, Pallas kernels, call(): pl.pallas_call(kernel, out_shape=tuple(outputs), in_specs=[vmem] * len(in...  5.77 us
  transfers between devices with their start and end apart: 10, of which 7 were waited for; matrix products, arithmetic and copies ran while one was open for 0% of the time, Pallas kernels for 5%

commit v1 on v0

--- a/solution.py
+++ b/solution.py
@@ -66,70 +66,146 @@
             store((2 * pair + 1) * wide + h, second)
 
 
-def pack_kernel(sigma_ref, out_ref):
-    copies, pieces = out_ref.shape[:2]
-    comps, rows = sigma_ref.shape[0], sigma_ref.shape[1] // 2
+def send_copies(source, out_ref, sent, index, span):
+    copies = [
+        pltpu.make_async_copy(source.at[span], out_ref.at[copy, span], sent.at[index, copy])
+        for copy in range(out_ref.shape[0])
+    ]
+    for copy in copies:
+        copy.start()
+    return copies
+
+
+def pack_kernel(sigma_ref, out_ref, rows_buffer, piece_buffer, arrived, sent):
+    comps, rows = rows_buffer.shape[:2]
+    per_orbital = piece_buffer.shape[0] // (comps // 2)
     mine = pl.ds(pl.multiple_of(lax.axis_index(CORE) * rows, 8), rows)
-
+    coming = [
+        pltpu.make_async_copy(sigma_ref.at[pl.ds(2 * o, 2), mine], rows_buffer.at[pl.ds(2 * o, 2)], arrived.at[o])
+        for o in range(comps // 2)
+    ]
+    for copy in coming:
+        copy.start()
+    going = []
     for orbital in range(comps // 2):
+        coming[orbital].wait()
 
         def store(index, tile, orbital=orbital):
-            for copy in range(copies):
-                out_ref[copy, orbital * (pieces // (comps // 2)) + index] = tile
-
-        store_packed(store, sigma_ref[2 * orbital, mine, :], sigma_ref[2 * orbital + 1, mine, :])
+            piece_buffer[orbital * per_orbital + index] = tile
+
+        store_packed(store, rows_buffer[2 * orbital], rows_buffer[2 * orbital + 1])
+        going += send_copies(piece_buffer, out_ref, sent, orbital, pl.ds(orbital * per_orbital, per_orbital))
+    for copy in going:
+        copy.wait()
 
 
 def pack(sigma, copies):
     comps, rows, cols = sigma.shape
     pieces = comps // 2 * (rows // 2) * cols // (SUB * LANES)
-    return call(pack_kernel, [sigma], [far_out((copies, pieces, 8, LANES))])[0]
-
-
-def split_kernel(history_ref, high_ref, low_ref, last_ref):
-    _, rows, cols = history_ref.shape
+    anywhere = pl.BlockSpec(memory_space=pl.ANY)
+    return pl.pallas_call(
+        pack_kernel,
+        out_shape=far_out((copies, pieces, 8, LANES)),
+        in_specs=[anywhere],
+        out_specs=anywhere,
+        scratch_shapes=[
+            pltpu.VMEM((comps, rows // 2, cols), jnp.float32),
+            pltpu.VMEM((pieces, 8, LANES), jnp.float32),
+            pltpu.SemaphoreType.DMA((comps // 2,)),
+            pltpu.SemaphoreType.DMA((comps // 2, copies)),
+        ],
+        compiler_params=pltpu.CompilerParams(vmem_limit_bytes=VMEM_LIMIT),
+        name="pack",
+    )(far(sigma))
+
+
+def split_kernel(resident, history_ref, *refs):
+    comps, rows, cols = history_ref.shape
+    orbitals = comps // 2
+    outs, last_ref = refs[: 2 * orbitals], refs[2 * orbitals]
+    away = [i for i in range(2 * orbitals) if i not in resident]
+    buffer, *scratch, arrived, sent, sent_last = refs[2 * orbitals + 1 :]
+    last_buffer = scratch.pop()
+    places = list(outs)
+    for i, ref in zip(away, scratch, strict=True):
+        places[i] = ref
     keep_rows = last_ref.shape[1]
-    col_ids = lax.axis_index("tm") * cols + lax.broadcasted_iota(jnp.int32, (rows, cols), 1)
-    keep = col_ids <= lax.broadcasted_iota(jnp.int32, (rows, cols), 0)
-    high, low = halves_of(jnp.where(keep, history_ref[0], 0.0))
-    high_ref[0] = high
-    low_ref[0] = low
+    chunk = arrived.shape[0]
+    step = rows // chunk
+    coming = []
+    for c in range(chunk):
+        span = (slice(None), pl.ds(c * step, step))
+        coming.append(pltpu.make_async_copy(history_ref.at[span], buffer.at[span], arrived.at[c]))
+        coming[-1].start()
+    col_ids = lax.axis_index("tm") * cols + lax.broadcasted_iota(jnp.int32, (16, cols), 1)
+    base_ids = lax.broadcasted_iota(jnp.int32, (16, cols), 0)
+    going = []
+    for c in range(chunk):
+        coming[c].wait()
+        for r in range(c * step, (c + 1) * step, 16):
+            keep = col_ids <= r + base_ids
+            for i in range(comps):
+                high, low = halves_of(jnp.where(keep, buffer[i, r : r + 16, :], 0.0))
+                places[2 * (i // 2)][i % 2, r : r + 16, :] = high
+                places[2 * (i // 2) + 1][i % 2, r : r + 16, :] = low
+        for n, i in enumerate(away):
+            span = (slice(None), pl.ds(c * step, step))
+            going.append(pltpu.make_async_copy(places[i].at[span], outs[i].at[span], sent.at[c, n]))
+            going[-1].start()
     start = rows - 2 * keep_rows + lax.axis_index(CORE) * keep_rows
-    row_ids = start + lax.broadcasted_iota(jnp.int32, (keep_rows, cols), 0)
-    mine = pl.ds(pl.multiple_of(start, 8), keep_rows)
-    last_ref[0] = jnp.where(col_ids[:keep_rows] <= row_ids, history_ref[0, mine, :], 0.0)
-
-
-def split(history, keep_rows):
+    for r in range(0, keep_rows, 8):
+        keep = col_ids[:8] <= start + r + base_ids[:8]
+        mine = pl.ds(pl.multiple_of(start + r, 8), 8)
+        for i in range(comps):
+            last_buffer[i, r : r + 8, :] = jnp.where(keep, buffer[i, mine, :], 0.0)
+    going.append(pltpu.make_async_copy(last_buffer, last_ref, sent_last))
+    going[-1].start()
+    for copy in going:
+        copy.wait()
+
+
+def split(history, keep_rows, resident):
     comps, rows, cols = history.shape
-    whole = pl.BlockSpec((1, rows, cols), lambda i: (i, 0, 0))
-    return pl.pallas_call(
-        split_kernel,
-        out_shape=(
-            far_out(history.shape, jnp.bfloat16),
-            far_out(history.shape, jnp.bfloat16),
-            far_out((comps, keep_rows, cols)),
-        ),
-        grid=(comps,),
-        in_specs=[whole],
-        out_specs=(whole, whole, pl.BlockSpec((1, keep_rows, cols), lambda i: (i, 0, 0))),
+    orbitals = comps // 2
+    chunk = 5 if rows % 80 == 0 else 1
+    part = (2, rows, cols)
+    places = [near_out if i in resident else far_out for i in range(2 * orbitals)]
+    specs = [pl.BlockSpec(memory_space=pltpu.VMEM if i in resident else pl.ANY) for i in range(2 * orbitals)]
+    anywhere = pl.BlockSpec(memory_space=pl.ANY)
+    *parts, last = pl.pallas_call(
+        functools.partial(split_kernel, resident),
+        out_shape=(*[place(part, jnp.bfloat16) for place in places], far_out((comps, keep_rows, cols))),
+        in_specs=[anywhere],
+        out_specs=(*specs, anywhere),
+        scratch_shapes=[
+            pltpu.VMEM(history.shape, jnp.float32),
+            *[pltpu.VMEM(part, jnp.bfloat16)] * (2 * orbitals - len(resident)),
+            pltpu.VMEM((comps, keep_rows, cols), jnp.float32),
+            pltpu.SemaphoreType.DMA((chunk,)),
+            pltpu.SemaphoreType.DMA((chunk, 2 * orbitals)),
+            pltpu.SemaphoreType.DMA(()),
+        ],
         compiler_params=pltpu.CompilerParams(vmem_limit_bytes=VMEM_LIMIT),
         name="split",
     )(far(history))
-
-
-def block_kernel(block, windows, stacked, step_size, *refs):
-    count = 4 + (1 if stacked else 2) + 2 * windows
-    factor_ref, sigma_ref, sources = refs[0], refs[1], refs[2 : 2 + count]
-    outs, buffers, arrived = refs[2 + count : -(count + 3)], refs[-(count + 3) : -3], refs[-3]
+    return parts, last
+
+
+def block_kernel(block, windows, stacked, step_size, factor_ref, sigma_ref, *refs):
+    near_keys, far_keys = part_keys()
+    held = dict(zip(near_keys, refs[: len(near_keys)], strict=True))
+    refs = refs[len(near_keys) :]
+    count = len(far_keys) + (1 if stacked else 2) + 2 * windows
+    sources, outs, buffers = refs[:count], refs[count : -(count + 3)], refs[-(count + 3) : -3]
+    arrived, sigma_scratch, joined = refs[-3:]
     piece_ref, outs = outs[-1], outs[:-1]
-    sigma_scratch, joined = refs[-2:]
-    highs, lows = buffers[:2], buffers[2:4]
-    previous = (buffers[4].at[0], buffers[4].at[1]) if stacked else buffers[4:6]
-    mine_refs, theirs_refs = buffers[-2 * windows : count - windows], buffers[count - windows :]
+    held.update(zip(far_keys, buffers[: len(far_keys)], strict=True))
+    rows_at = len(far_keys)
+    previous = (buffers[rows_at].at[0], buffers[rows_at].at[1]) if stacked else buffers[rows_at : rows_at + 2]
+    mine_refs, theirs_refs = buffers[count - 2 * windows : count - windows], buffers[count - windows :]
     comps, rows, cols = previous[0].shape
     orbitals = comps // 2
-    known_rows = highs[0].shape[1]
+    known_rows = held[far_keys[0]].shape[1]
     used = known_rows + windows * 2 * rows
     wide = cols // LANES
     per_orbital = piece_ref.shape[0] // orbitals
@@ -138,15 +214,17 @@
         span = pl.ds(2 * orbital, 2)
         return ref.at[span] if len(ref.shape) == 3 else ref.at[:, span]
 
-    copies = [
-        [
-            pltpu.make_async_copy(part_of(source, o), part_of(buffer, o), arrived.at[o, i])
-            for i, (source, buffer) in enumerate(zip(sources, buffers, strict=True))
-        ]
-        for o in range(orbitals)
-    ]
-    for of_orbital in copies:
-        for copy in of_orbital:
+    known_copies, row_copies = {}, []
+    for o in range(orbitals):
+        for i, key in enumerate(far_keys):
+            if key[1] == o:
+                known_copies[key] = pltpu.make_async_copy(sources[i], buffers[i], arrived.at[o, i])
+                known_copies[key].start()
+        row_copies.append([
+            pltpu.make_async_copy(part_of(sources[i], o), part_of(buffers[i], o), arrived.at[o, i])
+            for i in range(rows_at, count)
+        ])
+        for copy in row_copies[o]:
             copy.start()
     core = lax.axis_index(CORE)
     mine_at = pl.ds(pl.multiple_of(core * rows, 8), rows)
@@ -174,20 +252,24 @@
             lanes = slice(LANES * tile, LANES * tile + LANES)
             sigma_scratch[: 2 * rows, lanes] = high
             sigma_scratch[2 * rows :, lanes] = low
-        for copy in copies[orbital]:
+
+        for key, copy in known_copies.items():
+            if key[1] == orbital:
+                copy.wait()
+        for copy in row_copies[orbital]:
             copy.wait()
-
         totals = None
         for momentum in range(2):
+            keys = [(momentum, orbital, half) for half in range(2)]
             products = []
-            for part in range(2 * orbital, 2 * orbital + 2):
-                total = product(slice(0, known_rows), highs[momentum][part], lows[momentum][part])
+            for part in range(2):
+                products.append(product(slice(0, known_rows), held[keys[0]][part], held[keys[1]][part]))
+            for part in range(2):
                 for window in range(windows):
-                    joined[mine_at, :] = mine_refs[window][momentum, part]
-                    joined[theirs_at, :] = theirs_refs[window][1 - momentum, part]
+                    joined[mine_at, :] = mine_refs[window][momentum, 2 * orbital + part]
+                    joined[theirs_at, :] = theirs_refs[window][1 - momentum, 2 * orbital + part]
                     start = known_rows + window * 2 * rows
-                    total = total + product(slice(start, start + 2 * rows), *halves_of(joined[...]))
-                products.append(total)
+                    products[part] += product(slice(start, start + 2 * rows), *halves_of(joined[...]))
             by_real, by_imag = products
             x_re = previous[momentum][2 * orbital] + step_size * (by_real[:rows] - by_imag[rows:])
             x_im = previous[momentum][2 * orbital + 1] + step_size * (by_imag[:rows] + by_real[rows:])
@@ -206,17 +288,28 @@
         store_packed(store, *totals)
 
 
-def advance(block, last, step_size, sigma, factors, highs, lows, previous, mine, theirs):
-    comps, known_rows, cols = highs[0].shape
-    rows = factors.shape[2]
+RESIDENT = ((0, 1), (0,))
+
+
+def part_keys():
+    keys = [(m, o, half) for o in range(2) for m in range(2) for half in range(2)]
+    here = [key for key in keys if 2 * key[1] + key[2] in RESIDENT[key[0]]]
+    return here, [key for key in keys if key not in here]
+
+
+def advance(block, last, step_size, sigma, factors, known, previous, mine, theirs):
+    comps, rows, cols = previous[0].shape[-3:]
+    known_rows = known[0][0].shape[1]
     used = pl.cdiv(known_rows + len(mine) * 2 * rows, LANES) * LANES
-    sources = [*highs, *lows, *previous, *mine, *theirs]
+    near_keys, far_keys = part_keys()
+    part = lambda key: known[key[0]][2 * key[1] + key[2]]
+    sources = [*map(part, far_keys), *previous, *mine, *theirs]
     greens = [far_out((comps, rows, cols))] * 2 if last else [far_out((2, comps, rows, cols))]
     vmem = pl.BlockSpec(memory_space=pltpu.VMEM)
     *greens, pieces = pl.pallas_call(
         functools.partial(block_kernel, block, len(mine), len(previous) == 1, step_size),
         out_shape=(*greens, near_out((sigma.shape[1], 8, LANES))),
-        in_specs=[vmem, vmem] + [pl.BlockSpec(memory_space=pl.ANY)] * len(sources),
+        in_specs=[vmem] * (2 + len(near_keys)) + [pl.BlockSpec(memory_space=pl.ANY)] * len(sources),
         out_specs=(vmem,) * (len(greens) + 1),
         scratch_shapes=[
             *[pltpu.VMEM(source.shape, source.dtype) for source in sources],
@@ -225,7 +318,7 @@
             pltpu.VMEM((2 * rows, cols), jnp.float32),
         ],
         compiler_params=pltpu.CompilerParams(vmem_limit_bytes=VMEM_LIMIT),
-    )(factors, near(sigma), *[far(source) for source in sources])
+    )(factors, near(sigma), *[near(part(key)) for key in near_keys], *[far(source) for source in sources])
     return greens, pieces
 
 
@@ -247,13 +340,21 @@
     return call(kernel, [parts], [near_out(parts.shape)])[0]
 
 
-def copies_kernel(value_ref, out_ref):
-    for i in range(out_ref.shape[0]):
-        out_ref[i] = value_ref[...]
+def copies_kernel(value_ref, out_ref, sent):
+    for copy in send_copies(value_ref, out_ref, sent, 0, pl.ds(0, value_ref.shape[0])):
+        copy.wait()
 
 
 def copies_of(value, count):
-    return call(copies_kernel, [value], [far_out((count, *value.shape))])[0]
+    return pl.pallas_call(
+        copies_kernel,
+        out_shape=far_out((count, *value.shape)),
+        in_specs=[pl.BlockSpec(memory_space=pltpu.VMEM)],
+        out_specs=pl.BlockSpec(memory_space=pl.ANY),
+        scratch_shapes=[pltpu.SemaphoreType.DMA((1, count))],
+        compiler_params=pltpu.CompilerParams(vmem_limit_bytes=VMEM_LIMIT),
+        name="copies",
+    )(near(value))
 
 
 def green_kernel(mine_ref, theirs_ref, out_ref):
@@ -300,16 +401,14 @@
     sigma = lax.all_to_all(packed_first, "tm", 0, 0, tiled=True)
     their_history = swapped(history)
     their_propagator = swapped(propagator)
-    own = split(history, rows)
-    other = split(their_history, rows)
-    highs, lows, greens = (own[0], other[0]), (own[1], other[1]), (own[2], other[2])
+    known, greens = zip(split(history, rows, RESIDENT[0]), split(their_history, rows, RESIDENT[1]), strict=True)
     factors = jnp.stack([propagator, their_propagator]).reshape(2, comps // 2, 2, blocks, 2, rows)
     factors = lax.dynamic_index_in_dim(factors, core, 4, keepdims=False)
     factors = factors.transpose(3, 1, 4, 2, 0).reshape(blocks, comps // 2, rows, 4)
     mine, theirs = [], []
     for block in range(blocks):
         last = block + 1 == blocks
-        greens, pieces = advance(block, last, step_size, sigma, factors, highs, lows, greens, mine, theirs)
+        greens, pieces = advance(block, last, step_size, sigma, factors, known, greens, mine, theirs)
         parts = lax.all_to_all(pieces, YZ, 0, 0, tiled=True)
         sigma = lax.all_to_all(cube(parts, norm_factor), YZ, 0, 0, tiled=True)
         if not last:

time: 204 us -> 202 us (level)
  Pallas kernels: 29.5 us -> 25.7 us
  waiting for transfers between devices: 20 us -> 22.7 us
    pallas_call x8 -> x5, Pallas kernels: 5.77 us -> 2.52 us  [call(): pl.pallas_call(kernel, out_shape=tuple(outputs), in_specs=[vmem] * len(in...]
    all_to_all x1, waiting for transfers between devices: 4.29 us -> 7.2 us  [body(): sigma = lax.all_to_all(packed_first, 'tm', 0, 0, tiled=True)]
    pallas_call x2 -> x5, Pallas kernels: 8.5 us -> 9.58 us  [the longest x2 5.58 us: split(): pl.pallas_call(functools.partial(split_kernel, resident), out_shape=(*[pl...]
  transfers between devices with their start and end apart: 10 -> 10, of which waited for: 7 -> 6; matrix products, arithmetic and copies ran while one was open for 0% -> 0% of each run, Pallas kernels for 5% -> 4%
where the time goes in v1:
time: 202 us
  blocking collectives  97.1 us (48%)
  starting transfers between devices  53.9 us (27%)
  Pallas kernels  25.7 us (13%)
  waiting for transfers between devices  22.7 us (11%)
    all_to_all x3, blocking collectives, body(): parts = lax.all_to_all(pieces, YZ, 0, 0, tiled=True)  61.7 us
    ppermute x6, starting transfers between devices, swapped(): return lax.ppermute(value, CORE, [(0, 1), (1, 0)])  38.7 us
    all_to_all x2, blocking collectives, body(): sigma = lax.all_to_all(cube(parts, norm_factor), YZ, 0, 0, tiled=True)  35.4 us
    pallas_call x3, Pallas kernels, advance(): pl.pallas_call(functools.partial(block_kernel, block, len(mine), len(prev...  13.6 us
    all_to_all x1, waiting for transfers between devices, body(): sigma = lax.all_to_all(packed_first, 'tm', 0, 0, tiled=True)  7.2 us
    all_to_all x2, starting transfers between devices, body(): sigma = lax.all_to_all(copies_of(sigma, shards), 'tm', 0, 0, tiled=True)  7.05 us
    all_to_all x2, waiting for transfers between devices, body(): sigma = lax.all_to_all(copies_of(sigma, shards), 'tm', 0, 0, tiled=True)  7 us
    pallas_call x2, Pallas kernels, split(): pl.pallas_call(functools.partial(split_kernel, resident), out_shape=(*[pl...  5.58 us
  transfers between devices with their start and end apart: 10, of which 6 were waited for; matrix products, arithmetic and copies ran while one was open for 0% of the time, Pallas kernels for 4%

profile of v1, /device:TPU:1, one launch (start us, length us, event | category | flops | bytes accessed | tf_op | source)
XLA Modules:
  0.0 201.5 jit_solution(14371848167309870266)
XLA Ops:
  0.6 0.0 copy-start.1
  0.6 8.8 %collective-permute-start.1 = (f32[4,640,256]{2,1,0:T(8,128)}, f32[4,640,256]{2,1,0:T(8,128)}, u32[]{:S(2)}, u32[]{:S(2)}) collective-permute-start(f32[4,640,256]{2,1,0:T(8,128)} %bitcast.12), channel_id=1, source_target_pairs={{0,4},{4,0},{1,5},{5,1},{2,6},{6,2},{3,7},{7,3},{8,12},{12,8},{9,1... | collective-permute-start | bytes 7864328 | tf_op jit(solution)/shard_map/ppermute | solution.py:398
  9.4 2.0 pack.1
  11.4 3.5 %all-to-all-start = ((f32[4,64,8,128]{3,2,1,0:T(8,128)}), f32[4,64,8,128]{3,2,1,0:T(8,128)S(1)}, u32[]{:S(2)}, u32[]{:S(2)}) async-start(f32[4,64,8,128]{3,2,1,0:T(8,128)} %pack.1), calls=%async_computation | async-start | bytes 2097152 | tf_op jit(solution)/shard_map/all_to_all | solution.py:401
  14.9 0.0 copy-done.1
  14.9 1.9 collective-permute-start
  16.9 2.7 %split.2 = (bf16[2,640,256]{2,1,0:T(8,128)(2,1)S(1)}, bf16[2,640,256]{2,1,0:T(8,128)(2,1)S(1)}, bf16[2,640,256]{2,1,0:T(8,128)(2,1)}, bf16[2,640,256]{2,1,0:T(8,128)(2,1)}, f32[4,64,256]{2,1,0:T(8,128)}) custom-call(f32[4,640,256]{2,1,0:T(8,128)} %bitcast.13), custom_call_target="tpu_custom_call" | custom-call | tf_op jit(solution)/shard_map/split/pallas_call | solution.py:175
  19.6 0.1 stack.8
  19.7 0.0 collective-permute-done
  19.7 0.1 stack.9
  19.9 0.1 copy.10.factor_ref
  20.0 0.0 collective-permute-done.1.history_ref
  20.0 2.8 %split.3 = (bf16[2,640,256]{2,1,0:T(8,128)(2,1)S(1)}, bf16[2,640,256]{2,1,0:T(8,128)(2,1)}, bf16[2,640,256]{2,1,0:T(8,128)(2,1)}, bf16[2,640,256]{2,1,0:T(8,128)(2,1)}, f32[4,64,256]{2,1,0:T(8,128)}) custom-call(f32[4,640,256]{2,1,0:T(8,128)} %collective-permute-done.1.history_ref), custom_call_target="tpu_custom_call" | custom-call | tf_op jit(solution)/shard_map/split/pallas_call | solution.py:175
  22.9 7.2 %all-to-all-done.sigma_ref = f32[4,64,8,128]{3,2,1,0:T(8,128)S(1)} async-done(((f32[4,64,8,128]{3,2,1,0:T(8,128)}), f32[4,64,8,128]{3,2,1,0:T(8,128)S(1)}, u32[]{:S(2)}, u32[]{:S(2)}) %all-to-all-start) | async-done | bytes 1048608 | tf_op jit(solution)/shard_map/all_to_all | solution.py:401
  30.1 3.7 %shard_map.50 = (f32[2,4,64,256]{3,2,1,0:T(8,128)}, f32[64,8,128]{2,1,0:T(8,128)S(1)}) custom-call(f32[3,2,64,4]{3,2,1,0:T(8,128)S(1)} %copy.10.factor_ref, f32[4,64,8,128]{3,2,1,0:T(8,128)S(1)} %all-to-all-done.sigma_ref, bf16[2,640,256]{2,1,0:T(8,128)(2,1)S(1)} %get-tuple-element.19.refs_0_, bf16[2,640,256]{2,1,0:T(8,128)(2,1)S(1)} %get-tuple-element.20.refs_1_, ...), custom_call_target="tpu_custom_call" | custom-call | tf_op jit(solution)/shard_map/pallas_call | solution.py:309
  33.8 23.4 %all_to_all.45.parts_ref = f32[64,8,128]{2,1,0:T(8,128)S(1)} all-to-all(f32[64,8,128]{2,1,0:T(8,128)S(1)} %get-tuple-element.29), channel_id=1, replica_groups=mesh['mom_0'=8,'mom_1'=8,'core_of_chip'=2,'tm'=4] {'mom_0','mom_1'}, dimensions={0} | all-to-all | bytes 524288 | tf_op jit(solution)/shard_map/all_to_all | solution.py:412
  57.3 18.4 %all_to_all.46.value_ref = f32[64,8,128]{2,1,0:T(8,128)S(1)} all-to-all(f32[64,8,128]{2,1,0:T(8,128)S(1)} %shard_map.51), channel_id=1, replica_groups=mesh['mom_0'=8,'mom_1'=8,'core_of_chip'=2,'tm'=4] {'mom_0','mom_1'}, dimensions={0} | all-to-all | bytes 524288 | tf_op jit(solution)/shard_map/all_to_all | solution.py:413
  75.7 1.0 copies.2
  76.7 3.5 %all-to-all-start.3 = ((f32[4,64,8,128]{3,2,1,0:T(8,128)}), f32[4,64,8,128]{3,2,1,0:T(8,128)S(1)}, u32[]{:S(2)}, u32[]{:S(2)}) async-start(f32[4,64,8,128]{3,2,1,0:T(8,128)} %copies.2), calls=%async_computation.3 | async-start | bytes 2097152 | tf_op jit(solution)/shard_map/all_to_all | solution.py:417
  80.2 5.4 %collective-permute-start.2 = (f32[2,4,64,256]{3,2,1,0:T(8,128)}, f32[2,4,64,256]{3,2,1,0:T(8,128)}, u32[]{:S(2)}, u32[]{:S(2)}) collective-permute-start(f32[2,4,64,256]{3,2,1,0:T(8,128)} %get-tuple-element.30.refs_8_.refs_9_), channel_id=1, source_target_pairs={{0,4},{4,0},{1,5},{5,1},{2,6},{6,2},{3,7},{7,3},{8,12},{12,8},{9,1... | collective-permute-start | bytes 1572872 | tf_op jit(solution)/shard_map/ppermute | solution.py:398
  85.6 1.9 collective-permute-done.2.refs_10_.refs_11_
  87.5 4.1 %all-to-all-done.3.sigma_ref = f32[4,64,8,128]{3,2,1,0:T(8,128)S(1)} async-done(((f32[4,64,8,128]{3,2,1,0:T(8,128)}), f32[4,64,8,128]{3,2,1,0:T(8,128)S(1)}, u32[]{:S(2)}, u32[]{:S(2)}) %all-to-all-start.3) | async-done | bytes 1048608 | tf_op jit(solution)/shard_map/all_to_all | solution.py:417
  91.6 4.5 %shard_map.52 = (f32[2,4,64,256]{3,2,1,0:T(8,128)}, f32[64,8,128]{2,1,0:T(8,128)S(1)}) custom-call(f32[3,2,64,4]{3,2,1,0:T(8,128)S(1)} %copy.10.factor_ref, f32[4,64,8,128]{3,2,1,0:T(8,128)S(1)} %all-to-all-done.3.sigma_ref, bf16[2,640,256]{2,1,0:T(8,128)(2,1)S(1)} %get-tuple-element.19.refs_0_, bf16[2,640,256]{2,1,0:T(8,128)(2,1)S(1)} %get-tuple-element.20.refs_1_, ...), custom_call_target="tpu_custom_call" | custom-call | tf_op jit(solution)/shard_map/pallas_call | solution.py:309
  96.2 21.2 %all_to_all.47.parts_ref = f32[64,8,128]{2,1,0:T(8,128)S(1)} all-to-all(f32[64,8,128]{2,1,0:T(8,128)S(1)} %get-tuple-element.31), channel_id=1, replica_groups=mesh['mom_0'=8,'mom_1'=8,'core_of_chip'=2,'tm'=4] {'mom_0','mom_1'}, dimensions={0} | all-to-all | bytes 524288 | tf_op jit(solution)/shard_map/all_to_all | solution.py:412
  117.4 17.0 %all_to_all.48.value_ref = f32[64,8,128]{2,1,0:T(8,128)S(1)} all-to-all(f32[64,8,128]{2,1,0:T(8,128)S(1)} %shard_map.53), channel_id=1, replica_groups=mesh['mom_0'=8,'mom_1'=8,'core_of_chip'=2,'tm'=4] {'mom_0','mom_1'}, dimensions={0} | all-to-all | bytes 524288 | tf_op jit(solution)/shard_map/all_to_all | solution.py:413
  134.4 1.0 copies.3
  135.5 3.5 %all-to-all-start.6 = ((f32[4,64,8,128]{3,2,1,0:T(8,128)}), f32[4,64,8,128]{3,2,1,0:T(8,128)S(1)}, u32[]{:S(2)}, u32[]{:S(2)}) async-start(f32[4,64,8,128]{3,2,1,0:T(8,128)} %copies.3), calls=%async_computation.6 | async-start | bytes 2097152 | tf_op jit(solution)/shard_map/all_to_all | solution.py:417
  139.0 6.0 %collective-permute-start.3 = (f32[2,4,64,256]{3,2,1,0:T(8,128)}, f32[2,4,64,256]{3,2,1,0:T(8,128)}, u32[]{:S(2)}, u32[]{:S(2)}) collective-permute-start(f32[2,4,64,256]{3,2,1,0:T(8,128)} %get-tuple-element.32.refs_8_.refs_10_), channel_id=1, source_target_pairs={{0,4},{4,0},{1,5},{5,1},{2,6},{6,2},{3,7},{7,3},{8,12},{12,8},{9,1... | collective-permute-start | bytes 1572872 | tf_op jit(solution)/shard_map/ppermute | solution.py:398
  145.0 1.9 collective-permute-done.3.refs_12_
  146.9 2.9 %all-to-all-done.6.sigma_ref = f32[4,64,8,128]{3,2,1,0:T(8,128)S(1)} async-done(((f32[4,64,8,128]{3,2,1,0:T(8,128)}), f32[4,64,8,128]{3,2,1,0:T(8,128)S(1)}, u32[]{:S(2)}, u32[]{:S(2)}) %all-to-all-start.6) | async-done | bytes 1048608 | tf_op jit(solution)/shard_map/all_to_all | solution.py:417
  149.8 5.3 %shard_map.54 = (f32[4,64,256]{2,1,0:T(8,128)}, f32[4,64,256]{2,1,0:T(8,128)}, f32[64,8,128]{2,1,0:T(8,128)S(1)}) custom-call(f32[3,2,64,4]{3,2,1,0:T(8,128)S(1)} %copy.10.factor_ref, f32[4,64,8,128]{3,2,1,0:T(8,128)S(1)} %all-to-all-done.6.sigma_ref, bf16[2,640,256]{2,1,0:T(8,128)(2,1)S(1)} %get-tuple-element.19.refs_0_, ...), custom_call_target="tpu_custom_call" | custom-call | tf_op jit(solution)/shard_map/pallas_call | solution.py:309
  155.0 17.0 %all_to_all.49.parts_ref = f32[64,8,128]{2,1,0:T(8,128)S(1)} all-to-all(f32[64,8,128]{2,1,0:T(8,128)S(1)} %get-tuple-element.35), channel_id=1, replica_groups=mesh['mom_0'=8,'mom_1'=8,'core_of_chip'=2,'tm'=4] {'mom_0','mom_1'}, dimensions={0} | all-to-all | bytes 524288 | tf_op jit(solution)/shard_map/all_to_all | solution.py:412
  172.0 0.7 shard_map.56
  172.8 4.6 %all-to-all-start.8 = ((f32[64,8,128]{2,1,0:T(8,128)}), f32[64,8,128]{2,1,0:T(8,128)S(1)}, u32[]{:S(2)}, u32[]{:S(2)}) async-start(f32[64,8,128]{2,1,0:T(8,128)} %shard_map.56), calls=%async_computation.8 | async-start | bytes 524288 | tf_op jit(solution)/shard_map/all_to_all | solution.py:413
  177.4 7.8 %collective-permute-start.4 = (f32[4,64,256]{2,1,0:T(8,128)}, f32[4,64,256]{2,1,0:T(8,128)S(1)}, u32[]{:S(2)}, u32[]{:S(2)}) collective-permute-start(f32[4,64,256]{2,1,0:T(8,128)} %get-tuple-element.34), channel_id=1, source_target_pairs={{0,4},{4,0},{1,5},{5,1},{2,6},{6,2},{3,7},{7,3},{8,12},{12,8},{9,1... | collective-permute-start | bytes 786440 | tf_op jit(solution)/shard_map/ppermute | solution.py:398
  185.2 4.8 %all-to-all-done.8.mine_ref = f32[64,8,128]{2,1,0:T(8,128)S(1)} async-done(((f32[64,8,128]{2,1,0:T(8,128)}), f32[64,8,128]{2,1,0:T(8,128)S(1)}, u32[]{:S(2)}, u32[]{:S(2)}) %all-to-all-start.8) | async-done | bytes 262176 | tf_op jit(solution)/shard_map/all_to_all | solution.py:413
  190.0 8.9 %collective-permute-start.5 = (f32[64,8,128]{2,1,0:T(8,128)S(1)}, f32[64,8,128]{2,1,0:T(8,128)S(1)}, u32[]{:S(2)}, u32[]{:S(2)}) collective-permute-start(f32[64,8,128]{2,1,0:T(8,128)S(1)} %all-to-all-done.8.mine_ref), channel_id=1, source_target_pairs={{0,4},{4,0},{1,5},{5,1},{2,6},{6,2},{3,7},{7,3},{8,12},{12,8},{9,1... | collective-permute-start | bytes 786440 | tf_op jit(solution)/shard_map/ppermute | solution.py:398
  198.8 0.0 collective-permute-done.4.theirs_ref
  198.9 0.0 copy-start
  198.9 0.9 copy-done
  199.8 0.8 shard_map.55
  200.7 0.0 collective-permute-done.5.theirs_ref
  200.7 0.8 shard_map.57
  (6 shorter events, 0.2 us)
Async XLA Ops:
  0.6 14.3 %copy-start.1 = (f32[4,1,384]{2,1,0:T(1,128)S(1)}, f32[4,1,384]{2,1,0:T(1,128)}, u32[]{:S(2)}) copy-start(f32[4,1,384]{2,1,0:T(1,128)} %param.5) | copy-start | bytes 18436
  0.6 19.4 %collective-permute-start.1 = (f32[4,640,256]{2,1,0:T(8,128)}, f32[4,640,256]{2,1,0:T(8,128)}, u32[]{:S(2)}, u32[]{:S(2)}) collective-permute-start(f32[4,640,256]{2,1,0:T(8,128)} %bitcast.12), channel_id=1, source_target_pairs={{0,4},{4,0},{1,5},{5,1},{2,6},{6,2},{3,7},{7,3},{8,12},{12,8},{9,1... | collective-permute-start | bytes 7864328 | tf_op jit(solution)/shard_map/ppermute | solution.py:398
  11.4 18.7 %all-to-all-start = ((f32[4,64,8,128]{3,2,1,0:T(8,128)}), f32[4,64,8,128]{3,2,1,0:T(8,128)S(1)}, u32[]{:S(2)}, u32[]{:S(2)}) async-start(f32[4,64,8,128]{3,2,1,0:T(8,128)} %pack.1), calls=%async_computation | async-start | bytes 2097152 | tf_op jit(solution)/shard_map/all_to_all | solution.py:401
  14.9 4.8 %collective-permute-start = (f32[4,384]{1,0:T(4,128)S(1)}, f32[4,384]{1,0:T(4,128)S(1)}, u32[]{:S(2)}, u32[]{:S(2)}) collective-permute-start(f32[4,384]{1,0:T(4,128)S(1)} %bitcast.16), channel_id=1, source_target_pairs={{0,4},{4,0},{1,5},{5,1},{2,6},{6,2},{3,7},{7,3},{8,12},{12,8},{9,1... | collective-permute-start | bytes 18440 | tf_op jit(solution)/shard_map/ppermute | solution.py:398
  76.7 14.9 %all-to-all-start.3 = ((f32[4,64,8,128]{3,2,1,0:T(8,128)}), f32[4,64,8,128]{3,2,1,0:T(8,128)S(1)}, u32[]{:S(2)}, u32[]{:S(2)}) async-start(f32[4,64,8,128]{3,2,1,0:T(8,128)} %copies.2), calls=%async_computation.3 | async-start | bytes 2097152 | tf_op jit(solution)/shard_map/all_to_all | solution.py:417
  80.2 7.3 %collective-permute-start.2 = (f32[2,4,64,256]{3,2,1,0:T(8,128)}, f32[2,4,64,256]{3,2,1,0:T(8,128)}, u32[]{:S(2)}, u32[]{:S(2)}) collective-permute-start(f32[2,4,64,256]{3,2,1,0:T(8,128)} %get-tuple-element.30.refs_8_.refs_9_), channel_id=1, source_target_pairs={{0,4},{4,0},{1,5},{5,1},{2,6},{6,2},{3,7},{7,3},{8,12},{12,8},{9,1... | collective-permute-start | bytes 1572872 | tf_op jit(solution)/shard_map/ppermute | solution.py:398
  135.5 14.3 %all-to-all-start.6 = ((f32[4,64,8,128]{3,2,1,0:T(8,128)}), f32[4,64,8,128]{3,2,1,0:T(8,128)S(1)}, u32[]{:S(2)}, u32[]{:S(2)}) async-start(f32[4,64,8,128]{3,2,1,0:T(8,128)} %copies.3), calls=%async_computation.6 | async-start | bytes 2097152 | tf_op jit(solution)/shard_map/all_to_all | solution.py:417
  139.0 7.9 %collective-permute-start.3 = (f32[2,4,64,256]{3,2,1,0:T(8,128)}, f32[2,4,64,256]{3,2,1,0:T(8,128)}, u32[]{:S(2)}, u32[]{:S(2)}) collective-permute-start(f32[2,4,64,256]{3,2,1,0:T(8,128)} %get-tuple-element.32.refs_8_.refs_10_), channel_id=1, source_target_pairs={{0,4},{4,0},{1,5},{5,1},{2,6},{6,2},{3,7},{7,3},{8,12},{12,8},{9,1... | collective-permute-start | bytes 1572872 | tf_op jit(solution)/shard_map/ppermute | solution.py:398
  172.8 17.2 %all-to-all-start.8 = ((f32[64,8,128]{2,1,0:T(8,128)}), f32[64,8,128]{2,1,0:T(8,128)S(1)}, u32[]{:S(2)}, u32[]{:S(2)}) async-start(f32[64,8,128]{2,1,0:T(8,128)} %shard_map.56), calls=%async_computation.8 | async-start | bytes 524288 | tf_op jit(solution)/shard_map/all_to_all | solution.py:413
  177.4 21.4 %collective-permute-start.4 = (f32[4,64,256]{2,1,0:T(8,128)}, f32[4,64,256]{2,1,0:T(8,128)S(1)}, u32[]{:S(2)}, u32[]{:S(2)}) collective-permute-start(f32[4,64,256]{2,1,0:T(8,128)} %get-tuple-element.34), channel_id=1, source_target_pairs={{0,4},{4,0},{1,5},{5,1},{2,6},{6,2},{3,7},{7,3},{8,12},{12,8},{9,1... | collective-permute-start | bytes 786440 | tf_op jit(solution)/shard_map/ppermute | solution.py:398
  190.0 10.7 %collective-permute-start.5 = (f32[64,8,128]{2,1,0:T(8,128)S(1)}, f32[64,8,128]{2,1,0:T(8,128)S(1)}, u32[]{:S(2)}, u32[]{:S(2)}) collective-permute-start(f32[64,8,128]{2,1,0:T(8,128)S(1)} %all-to-all-done.8.mine_ref), channel_id=1, source_target_pairs={{0,4},{4,0},{1,5},{5,1},{2,6},{6,2},{3,7},{7,3},{8,12},{12,8},{9,1... | collective-permute-start | bytes 786440 | tf_op jit(solution)/shard_map/ppermute | solution.py:398
  198.9 1.0 copy-start

commit v2 on v1

--- a/solution.py
+++ b/solution.py
@@ -1,4 +1,5 @@
 import functools
+import math
 
 import jax
 import jax.numpy as jnp
@@ -76,7 +77,7 @@
     return copies
 
 
-def pack_kernel(sigma_ref, out_ref, rows_buffer, piece_buffer, arrived, sent):
+def pack_kernel(sigma_ref, out_ref, piece_buffer, rows_buffer, arrived, sent):
     comps, rows = rows_buffer.shape[:2]
     per_orbital = piece_buffer.shape[0] // (comps // 2)
     mine = pl.ds(pl.multiple_of(lax.axis_index(CORE) * rows, 8), rows)
@@ -105,12 +106,11 @@
     anywhere = pl.BlockSpec(memory_space=pl.ANY)
     return pl.pallas_call(
         pack_kernel,
-        out_shape=far_out((copies, pieces, 8, LANES)),
+        out_shape=(far_out((copies, pieces, 8, LANES)), near_out((pieces, 8, LANES))),
         in_specs=[anywhere],
-        out_specs=anywhere,
+        out_specs=(anywhere, pl.BlockSpec(memory_space=pltpu.VMEM)),
         scratch_shapes=[
             pltpu.VMEM((comps, rows // 2, cols), jnp.float32),
-            pltpu.VMEM((pieces, 8, LANES), jnp.float32),
             pltpu.SemaphoreType.DMA((comps // 2,)),
             pltpu.SemaphoreType.DMA((comps // 2, copies)),
         ],
@@ -121,14 +121,9 @@
 
 def split_kernel(resident, history_ref, *refs):
     comps, rows, cols = history_ref.shape
-    orbitals = comps // 2
-    outs, last_ref = refs[: 2 * orbitals], refs[2 * orbitals]
-    away = [i for i in range(2 * orbitals) if i not in resident]
-    buffer, *scratch, arrived, sent, sent_last = refs[2 * orbitals + 1 :]
-    last_buffer = scratch.pop()
-    places = list(outs)
-    for i, ref in zip(away, scratch, strict=True):
-        places[i] = ref
+    count = 2 * (comps // 2)
+    outs, last_ref, held = refs[:count], refs[count], refs[count + 1 : count + 1 + len(resident)]
+    buffer, *places, last_buffer, arrived, sent, sent_last = refs[count + 1 + len(resident) :]
     keep_rows = last_ref.shape[1]
     chunk = arrived.shape[0]
     step = rows // chunk
@@ -145,12 +140,14 @@
         for r in range(c * step, (c + 1) * step, 16):
             keep = col_ids <= r + base_ids
             for i in range(comps):
-                high, low = halves_of(jnp.where(keep, buffer[i, r : r + 16, :], 0.0))
-                places[2 * (i // 2)][i % 2, r : r + 16, :] = high
-                places[2 * (i // 2) + 1][i % 2, r : r + 16, :] = low
-        for n, i in enumerate(away):
+                for n, value in enumerate(halves_of(jnp.where(keep, buffer[i, r : r + 16, :], 0.0))):
+                    part = 2 * (i // 2) + n
+                    places[part][i % 2, r : r + 16, :] = value
+                    if part in resident and r >= cols:
+                        held[resident.index(part)][i % 2, r - cols : r - cols + 16, :] = value
+        for i in range(count):
             span = (slice(None), pl.ds(c * step, step))
-            going.append(pltpu.make_async_copy(places[i].at[span], outs[i].at[span], sent.at[c, n]))
+            going.append(pltpu.make_async_copy(places[i].at[span], outs[i].at[span], sent.at[c, i]))
             going[-1].start()
     start = rows - 2 * keep_rows + lax.axis_index(CORE) * keep_rows
     for r in range(0, keep_rows, 8):
@@ -166,113 +163,200 @@
 
 def split(history, keep_rows, resident):
     comps, rows, cols = history.shape
-    orbitals = comps // 2
+    count = 2 * (comps // 2)
     chunk = 5 if rows % 80 == 0 else 1
-    part = (2, rows, cols)
-    places = [near_out if i in resident else far_out for i in range(2 * orbitals)]
-    specs = [pl.BlockSpec(memory_space=pltpu.VMEM if i in resident else pl.ANY) for i in range(2 * orbitals)]
+    part, later = (2, rows, cols), (2, rows - cols, cols)
     anywhere = pl.BlockSpec(memory_space=pl.ANY)
-    *parts, last = pl.pallas_call(
+    outs = pl.pallas_call(
         functools.partial(split_kernel, resident),
-        out_shape=(*[place(part, jnp.bfloat16) for place in places], far_out((comps, keep_rows, cols))),
+        out_shape=(
+            *[far_out(part, jnp.bfloat16)] * count,
+            far_out((comps, keep_rows, cols)),
+            *[near_out(later, jnp.bfloat16)] * len(resident),
+        ),
         in_specs=[anywhere],
-        out_specs=(*specs, anywhere),
+        out_specs=(*[anywhere] * (count + 1), *[pl.BlockSpec(memory_space=pltpu.VMEM)] * len(resident)),
         scratch_shapes=[
             pltpu.VMEM(history.shape, jnp.float32),
-            *[pltpu.VMEM(part, jnp.bfloat16)] * (2 * orbitals - len(resident)),
+            *[pltpu.VMEM(part, jnp.bfloat16)] * count,
             pltpu.VMEM((comps, keep_rows, cols), jnp.float32),
             pltpu.SemaphoreType.DMA((chunk,)),
-            pltpu.SemaphoreType.DMA((chunk, 2 * orbitals)),
+            pltpu.SemaphoreType.DMA((chunk, count)),
             pltpu.SemaphoreType.DMA(()),
         ],
         compiler_params=pltpu.CompilerParams(vmem_limit_bytes=VMEM_LIMIT),
         name="split",
     )(far(history))
-    return parts, last
-
-
-def block_kernel(block, windows, stacked, step_size, factor_ref, sigma_ref, *refs):
+    return outs[:count], outs[count], dict(zip(resident, outs[count + 1 :], strict=True))
+
+
+def unpack(load, scratch, rows, tile, lanes, wide, drop=None):
+    top = lax.broadcasted_iota(jnp.int32, (8, LANES), 0) < SUB
+    reals, imags = [], []
+    for pair in range(rows // 8):
+        first = load((2 * pair) * wide + tile % wide)
+        second = load((2 * pair + 1) * wide + tile % wide)
+        reals.append(jnp.where(top, first, jnp.roll(second, SUB, 0)))
+        imags.append(jnp.where(top, jnp.roll(first, SUB, 0), second))
+    value = jnp.concatenate(reals + imags, 0)
+    if drop is not None:
+        value = jnp.where(drop, 0.0, value)
+    high, low = halves_of(value)
+    scratch[: 2 * rows, lanes] = high
+    scratch[2 * rows :, lanes] = low
+
+
+def product(scratch, rows, span, high, low):
+    both = jnp.dot(scratch[:, span], high, preferred_element_type=jnp.float32)
+    rest = jnp.dot(scratch[: 2 * rows, span], low, preferred_element_type=jnp.float32)
+    return both[: 2 * rows] + (both[2 * rows :] + rest)
+
+
+def combined(by_real, by_imag, rows):
+    return by_real[:rows] - by_imag[rows:], by_imag[:rows] + by_real[rows:]
+
+
+def begin_kernel(stacked, step_size, sigma_ref, *refs):
+    sources, refs = refs[:8], refs[8:]
+    row_sources, refs = (refs[:1], refs[1:]) if stacked else (refs[:2], refs[2:])
+    out_ref, buffers, row_buffer, sigma_scratch, arrived, rows_arrived = refs[0], refs[1:9], *refs[9:]
+    _, comps, rows, cols = row_buffer.shape
+    known_rows = sources[0].shape[1]
+    piece = math.gcd(known_rows, cols)
+    wide = cols // LANES
+    per_orbital = sigma_ref.shape[0] // (comps // 2)
+    first_row = lax.axis_index("tm") * cols
+    if stacked:
+        row_copies = [pltpu.make_async_copy(row_sources[0], row_buffer, rows_arrived.at[0])]
+    else:
+        row_copies = [
+            pltpu.make_async_copy(source, row_buffer.at[m], rows_arrived.at[m]) for m, source in enumerate(row_sources)
+        ]
+    for copy in row_copies:
+        copy.start()
+
+    def copy_of(i, c):
+        at = pl.ds(pl.multiple_of(first_row + c * piece, 16), piece)
+        return pltpu.make_async_copy(sources[i].at[:, at], buffers[i].at[:, pl.ds(c * piece, piece)], arrived.at[i, c])
+
+    for c in range(cols // piece):
+        inside = first_row + c * piece < known_rows
+
+        @pl.when(inside)
+        def _(c=c):
+            for i in range(8):
+                copy_of(i, c).start()
+
+        @pl.when(jnp.logical_not(inside))
+        def _(c=c):
+            for i in range(8):
+                buffers[i][:, c * piece : (c + 1) * piece, :] = jnp.zeros((2, piece, cols), jnp.bfloat16)
+
+    for c in range(cols // piece):
+
+        @pl.when(first_row + c * piece < known_rows)
+        def _(c=c):
+            for i in range(8):
+                copy_of(i, c).wait()
+
+    for copy in row_copies:
+        copy.wait()
+    for orbital in range(comps // 2):
+        for tile in range(wide):
+            lanes = slice(LANES * tile, LANES * tile + LANES)
+            unpack(lambda i, at=orbital * per_orbital: sigma_ref[at + i], sigma_scratch, rows, tile, lanes, wide)
+        for momentum in range(2):
+            high, low = buffers[4 * momentum + 2 * orbital : 4 * momentum + 2 * orbital + 2]
+            products = [product(sigma_scratch, rows, slice(0, cols), high[part], low[part]) for part in range(2)]
+            for part, value in enumerate(combined(*products, rows)):
+                i = 2 * orbital + part
+                out_ref[momentum, i] = row_buffer[momentum, i] + step_size * value
+
+
+def begin(step_size, sigma, known, previous):
+    comps, rows, cols = previous[0].shape[-3:]
+    sources = [array for parts in known for array in parts]
+    anywhere, vmem = pl.BlockSpec(memory_space=pl.ANY), pl.BlockSpec(memory_space=pltpu.VMEM)
+    return pl.pallas_call(
+        functools.partial(begin_kernel, len(previous) == 1, step_size),
+        out_shape=far_out((2, comps, rows, cols)),
+        in_specs=[vmem, *[anywhere] * (len(sources) + len(previous))],
+        out_specs=vmem,
+        scratch_shapes=[
+            *[pltpu.VMEM((2, cols, cols), jnp.bfloat16)] * len(sources),
+            pltpu.VMEM((2, comps, rows, cols), jnp.float32),
+            pltpu.VMEM((4 * rows, cols), jnp.bfloat16),
+            pltpu.SemaphoreType.DMA((len(sources), cols // math.gcd(sources[0].shape[1], cols))),
+            pltpu.SemaphoreType.DMA((2,)),
+        ],
+        compiler_params=pltpu.CompilerParams(vmem_limit_bytes=VMEM_LIMIT),
+        name="begin",
+    )(near(sigma), *[far(value) for value in (*sources, *previous)])
+
+
+def block_kernel(block, windows, known_rows, step_size, factor_ref, sigma_ref, *refs):
     near_keys, far_keys = part_keys()
     held = dict(zip(near_keys, refs[: len(near_keys)], strict=True))
     refs = refs[len(near_keys) :]
-    count = len(far_keys) + (1 if stacked else 2) + 2 * windows
+    count = len(far_keys) + 1 + 2 * windows
     sources, outs, buffers = refs[:count], refs[count : -(count + 3)], refs[-(count + 3) : -3]
     arrived, sigma_scratch, joined = refs[-3:]
     piece_ref, outs = outs[-1], outs[:-1]
     held.update(zip(far_keys, buffers[: len(far_keys)], strict=True))
     rows_at = len(far_keys)
-    previous = (buffers[rows_at].at[0], buffers[rows_at].at[1]) if stacked else buffers[rows_at : rows_at + 2]
+    base_ref = buffers[rows_at]
     mine_refs, theirs_refs = buffers[count - 2 * windows : count - windows], buffers[count - windows :]
-    comps, rows, cols = previous[0].shape
+    _, comps, rows, cols = base_ref.shape
     orbitals = comps // 2
-    known_rows = held[far_keys[0]].shape[1]
     used = known_rows + windows * 2 * rows
     wide = cols // LANES
     per_orbital = piece_ref.shape[0] // orbitals
-
-    def part_of(ref, orbital):
-        span = pl.ds(2 * orbital, 2)
-        return ref.at[span] if len(ref.shape) == 3 else ref.at[:, span]
-
-    known_copies, row_copies = {}, []
+    copies = []
     for o in range(orbitals):
-        for i, key in enumerate(far_keys):
-            if key[1] == o:
-                known_copies[key] = pltpu.make_async_copy(sources[i], buffers[i], arrived.at[o, i])
-                known_copies[key].start()
-        row_copies.append([
-            pltpu.make_async_copy(part_of(sources[i], o), part_of(buffers[i], o), arrived.at[o, i])
+        copies.append([
+            pltpu.make_async_copy(sources[i].at[:, pl.ds(cols, known_rows - cols)], buffers[i], arrived.at[o, i])
+            for i, key in enumerate(far_keys)
+            if key[1] == o
+        ] + [
+            pltpu.make_async_copy(sources[i].at[:, pl.ds(2 * o, 2)], buffers[i].at[:, pl.ds(2 * o, 2)], arrived.at[o, i])
             for i in range(rows_at, count)
         ])
-        for copy in row_copies[o]:
+        for copy in copies[o]:
             copy.start()
-    core = lax.axis_index(CORE)
+    core, here = lax.axis_index(CORE), lax.axis_index("tm")
     mine_at = pl.ds(pl.multiple_of(core * rows, 8), rows)
     theirs_at = pl.ds(pl.multiple_of((1 - core) * rows, 8), rows)
-    top = lax.broadcasted_iota(jnp.int32, (8, LANES), 0) < SUB
     row_ids = known_rows + block * 2 * rows + core * rows + lax.broadcasted_iota(jnp.int32, (rows, cols), 0)
-    keep = lax.axis_index("tm") * cols + lax.broadcasted_iota(jnp.int32, (rows, cols), 1) <= row_ids
-
-    def product(span, high, low):
-        both = jnp.dot(sigma_scratch[:, span], high, preferred_element_type=jnp.float32)
-        rest = jnp.dot(sigma_scratch[: 2 * rows, span], low, preferred_element_type=jnp.float32)
-        return both[: 2 * rows] + (both[2 * rows :] + rest)
+    keep = here * cols + lax.broadcasted_iota(jnp.int32, (rows, cols), 1) <= row_ids
 
     for orbital in range(orbitals):
         base = orbital * per_orbital
-        for tile in range(pl.cdiv(used, LANES)):
-            shard, h = tile // wide, tile % wide
-            reals, imags = [], []
-            for pair in range(rows // 8):
-                first = sigma_ref[shard, base + (2 * pair) * wide + h]
-                second = sigma_ref[shard, base + (2 * pair + 1) * wide + h]
-                reals.append(jnp.where(top, first, jnp.roll(second, SUB, 0)))
-                imags.append(jnp.where(top, jnp.roll(first, SUB, 0), second))
-            high, low = halves_of(jnp.concatenate(reals + imags, 0))
-            lanes = slice(LANES * tile, LANES * tile + LANES)
-            sigma_scratch[: 2 * rows, lanes] = high
-            sigma_scratch[2 * rows :, lanes] = low
-
-        for key, copy in known_copies.items():
-            if key[1] == orbital:
-                copy.wait()
-        for copy in row_copies[orbital]:
+        for tile in range(wide, pl.cdiv(used, LANES)):
+            start, shard = LANES * tile, tile // wide
+            drop = None
+            if start < known_rows:
+                ids = start + lax.broadcasted_iota(jnp.int32, (4 * rows // 2, LANES), 1)
+                drop = jnp.logical_and(here == shard, ids < known_rows)
+            lanes = slice(start - cols, start - cols + LANES)
+            unpack(lambda i, at=base, j=shard: sigma_ref[j, at + i], sigma_scratch, rows, tile, lanes, wide, drop)
+        for copy in copies[orbital]:
             copy.wait()
+
         totals = None
         for momentum in range(2):
-            keys = [(momentum, orbital, half) for half in range(2)]
             products = []
             for part in range(2):
-                products.append(product(slice(0, known_rows), held[keys[0]][part], held[keys[1]][part]))
-            for part in range(2):
+                high, low = (held[momentum, orbital, half][part] for half in range(2))
+                total = product(sigma_scratch, rows, slice(0, known_rows - cols), high, low)
                 for window in range(windows):
                     joined[mine_at, :] = mine_refs[window][momentum, 2 * orbital + part]
                     joined[theirs_at, :] = theirs_refs[window][1 - momentum, 2 * orbital + part]
-                    start = known_rows + window * 2 * rows
-                    products[part] += product(slice(start, start + 2 * rows), *halves_of(joined[...]))
-            by_real, by_imag = products
-            x_re = previous[momentum][2 * orbital] + step_size * (by_real[:rows] - by_imag[rows:])
-            x_im = previous[momentum][2 * orbital + 1] + step_size * (by_imag[:rows] + by_real[rows:])
+                    start = known_rows - cols + window * 2 * rows
+                    total += product(sigma_scratch, rows, slice(start, start + 2 * rows), *halves_of(joined[...]))
+                products.append(total)
+            real, imag = combined(*products, rows)
+            x_re = base_ref[momentum, 2 * orbital] + step_size * real
+            x_im = base_ref[momentum, 2 * orbital + 1] + step_size * imag
             p_re = factor_ref[block, orbital, :, momentum : momentum + 1]
             p_im = factor_ref[block, orbital, :, 2 + momentum : 3 + momentum]
             real = jnp.where(keep, p_re * x_re - p_im * x_im, 0.0)
@@ -288,7 +372,7 @@
         store_packed(store, *totals)
 
 
-RESIDENT = ((0, 1), (0,))
+RESIDENT = ((0, 1, 2), (0, 1))
 
 
 def part_keys():
@@ -297,28 +381,30 @@
     return here, [key for key in keys if key not in here]
 
 
-def advance(block, last, step_size, sigma, factors, known, previous, mine, theirs):
-    comps, rows, cols = previous[0].shape[-3:]
+def advance(block, last, step_size, sigma, factors, known, held, base, mine, theirs):
+    _, comps, rows, cols = base.shape
     known_rows = known[0][0].shape[1]
     used = pl.cdiv(known_rows + len(mine) * 2 * rows, LANES) * LANES
     near_keys, far_keys = part_keys()
-    part = lambda key: known[key[0]][2 * key[1] + key[2]]
-    sources = [*map(part, far_keys), *previous, *mine, *theirs]
+    far_parts = [known[m][2 * o + half] for m, o, half in far_keys]
+    near_parts = [held[m][2 * o + half] for m, o, half in near_keys]
+    sources = [*far_parts, base, *mine, *theirs]
     greens = [far_out((comps, rows, cols))] * 2 if last else [far_out((2, comps, rows, cols))]
     vmem = pl.BlockSpec(memory_space=pltpu.VMEM)
     *greens, pieces = pl.pallas_call(
-        functools.partial(block_kernel, block, len(mine), len(previous) == 1, step_size),
+        functools.partial(block_kernel, block, len(mine), known_rows, step_size),
         out_shape=(*greens, near_out((sigma.shape[1], 8, LANES))),
         in_specs=[vmem] * (2 + len(near_keys)) + [pl.BlockSpec(memory_space=pl.ANY)] * len(sources),
         out_specs=(vmem,) * (len(greens) + 1),
         scratch_shapes=[
-            *[pltpu.VMEM(source.shape, source.dtype) for source in sources],
+            *[pltpu.VMEM((2, known_rows - cols, cols), jnp.bfloat16)] * len(far_parts),
+            *[pltpu.VMEM(source.shape, source.dtype) for source in sources[len(far_parts) :]],
             pltpu.SemaphoreType.DMA((comps // 2, len(sources))),
-            pltpu.VMEM((4 * rows, used), jnp.bfloat16),
+            pltpu.VMEM((4 * rows, used - cols), jnp.bfloat16),
             pltpu.VMEM((2 * rows, cols), jnp.float32),
         ],
         compiler_params=pltpu.CompilerParams(vmem_limit_bytes=VMEM_LIMIT),
-    )(factors, near(sigma), *[near(part(key)) for key in near_keys], *[far(source) for source in sources])
+    )(factors, near(sigma), *map(near, near_parts), *map(far, sources))
     return greens, pieces
 
 
@@ -397,27 +483,29 @@
     def swapped(value):
         return lax.ppermute(value, CORE, [(0, 1), (1, 0)])
 
-    packed_first = pack(sigma_first, shards)
+    packed_first, sigma_cols = pack(sigma_first, shards)
     sigma = lax.all_to_all(packed_first, "tm", 0, 0, tiled=True)
     their_history = swapped(history)
     their_propagator = swapped(propagator)
-    known, greens = zip(split(history, rows, RESIDENT[0]), split(their_history, rows, RESIDENT[1]), strict=True)
+    known, greens, held = zip(split(history, rows, RESIDENT[0]), split(their_history, rows, RESIDENT[1]), strict=True)
     factors = jnp.stack([propagator, their_propagator]).reshape(2, comps // 2, 2, blocks, 2, rows)
     factors = lax.dynamic_index_in_dim(factors, core, 4, keepdims=False)
     factors = factors.transpose(3, 1, 4, 2, 0).reshape(blocks, comps // 2, rows, 4)
     mine, theirs = [], []
     for block in range(blocks):
         last = block + 1 == blocks
-        greens, pieces = advance(block, last, step_size, sigma, factors, known, greens, mine, theirs)
+        base = begin(step_size, sigma_cols, known, greens)
+        greens, pieces = advance(block, last, step_size, sigma, factors, known, held, base, mine, theirs)
         parts = lax.all_to_all(pieces, YZ, 0, 0, tiled=True)
-        sigma = lax.all_to_all(cube(parts, norm_factor), YZ, 0, 0, tiled=True)
+        sigma_cols = lax.all_to_all(cube(parts, norm_factor), YZ, 0, 0, tiled=True)
         if not last:
             mine.append(greens[0])
             theirs.append(swapped(greens[0]))
-            sigma = lax.all_to_all(copies_of(sigma, shards), "tm", 0, 0, tiled=True)
+            sigma = lax.all_to_all(copies_of(sigma_cols, shards), "tm", 0, 0, tiled=True)
     whole = [far_out((comps, rows_block, cols))]
     green_last = call(green_kernel, [greens[0], swapped(greens[1])], whole)[0]
-    sigma_next = call(sigma_kernel, [sigma, swapped(sigma)], whole)[0]
+    green_last, sigma_cols = lax.optimization_barrier((green_last, sigma_cols))
+    sigma_next = call(sigma_kernel, [sigma_cols, swapped(sigma_cols)], whole)[0]
     return green_last[:, None], sigma_next
 
 

time: 202 us -> 200 us (0.990)
  waiting for transfers between devices: 22.7 us -> 11.7 us
  Pallas kernels: 25.7 us -> 33.9 us
    pallas_call x6 -> x9, Pallas kernels: 21.1 us -> 29.4 us  [the longest x3 11.6 us: advance(): pl.pallas_call(functools.partial(block_kernel, block, len(mine), known_ro...]
    all_to_all x3, waiting for transfers between devices: 11.8 us -> 5.61 us  [the longest x2 4.04 us: body(): lax.all_to_all(copies_of(sigma_cols, shards), 'tm', 0, 0, tiled=True)]
    all_to_all x1, waiting for transfers between devices: 7.2 us -> 3.59 us  [body(): sigma = lax.all_to_all(packed_first, 'tm', 0, 0, tiled=True)]
  transfers between devices with their start and end apart: 10 -> 10, of which waited for: 6 -> 6; matrix products, arithmetic and copies ran while one was open for 0% -> 0% of each run, Pallas kernels for 4% -> 9%
where the time goes in v2:
time: 200 us; the launch traced here: 199 us
  blocking collectives  97 us (48%)
  starting transfers between devices  54.1 us (27%)
  Pallas kernels  33.9 us (17%)
  waiting for transfers between devices  11.7 us (6%)
    all_to_all x3, blocking collectives, body(): parts = lax.all_to_all(pieces, YZ, 0, 0, tiled=True)  61.6 us
    ppermute x6, starting transfers between devices, swapped(): return lax.ppermute(value, CORE, [(0, 1), (1, 0)])  38.9 us
    all_to_all x2, blocking collectives, body(): sigma_cols = lax.all_to_all(cube(parts, norm_factor), YZ, 0, 0, tiled=True)  35.4 us
    pallas_call x3, Pallas kernels, advance(): pl.pallas_call(functools.partial(block_kernel, block, len(mine), known_ro...  11.6 us
    pallas_call x3, Pallas kernels, begin(): pl.pallas_call(functools.partial(begin_kernel, len(previous) == 1, step_s...  9.97 us
    all_to_all x2, starting transfers between devices, body(): lax.all_to_all(copies_of(sigma_cols, shards), 'tm', 0, 0, tiled=True)  7.05 us
    pallas_call x2, Pallas kernels, split(): pl.pallas_call(functools.partial(split_kernel, resident), out_shape=(*[fa...  5.86 us
    all_to_all x1, starting transfers between devices, body(): sigma_cols = lax.all_to_all(cube(parts, norm_factor), YZ, 0, 0, tiled=True)  4.62 us
  transfers between devices with their start and end apart: 10, of which 6 were waited for; matrix products, arithmetic and copies ran while one was open for 0% of the time, Pallas kernels for 9%

profile of v2, /device:TPU:1, one launch (start us, length us, event | category | flops | bytes accessed | tf_op | source)
XLA Modules:
  0.0 198.9 jit_solution(1651758068394813483)
XLA Ops:
  0.6 0.0 copy-start.1
  0.6 8.8 %collective-permute-start.1 = (f32[4,640,256]{2,1,0:T(8,128)}, f32[4,640,256]{2,1,0:T(8,128)}, u32[]{:S(2)}, u32[]{:S(2)}) collective-permute-start(f32[4,640,256]{2,1,0:T(8,128)} %bitcast.12), channel_id=1, source_target_pairs={{0,4},{4,0},{1,5},{5,1},{2,6},{6,2},{3,7},{7,3},{8,12},{12,8},{9,1... | collective-permute-start | bytes 7864328 | tf_op jit(solution)/shard_map/ppermute | solution.py:484
  9.4 2.0 pack.1
  11.4 3.5 %all-to-all-start = ((f32[4,64,8,128]{3,2,1,0:T(8,128)}), f32[4,64,8,128]{3,2,1,0:T(8,128)S(1)}, u32[]{:S(2)}, u32[]{:S(2)}) async-start(f32[4,64,8,128]{3,2,1,0:T(8,128)} %get-tuple-element.28), calls=%async_computation | async-start | bytes 2097152 | tf_op jit(solution)/shard_map/all_to_all | solution.py:487
  14.9 0.0 copy-done.1
  14.9 1.9 collective-permute-start
  16.9 2.9 %split.2 = (bf16[2,640,256]{2,1,0:T(8,128)(2,1)}, bf16[2,640,256]{2,1,0:T(8,128)(2,1)}, bf16[2,640,256]{2,1,0:T(8,128)(2,1)}, bf16[2,640,256]{2,1,0:T(8,128)(2,1...) custom-call(f32[4,640,256]{2,1,0:T(8,128)} %bitcast.13), custom_call_target="tpu_custom_call" | custom-call | tf_op jit(solution)/shard_map/split/pallas_call | solution.py:170
  19.8 0.1 stack.8
  19.8 0.0 collective-permute-done
  19.9 0.1 stack.9
  20.0 0.1 copy.10.factor_ref
  20.1 0.0 collective-permute-done.1.history_ref
  20.1 3.0 %split.3 = (bf16[2,640,256]{2,1,0:T(8,128)(2,1)}, bf16[2,640,256]{2,1,0:T(8,128)(2,1)}, bf16[2,640,256]{2,1,0:T(8,128)(2,1)}, bf16[2,640,256]{2,1,0:T(8,128)(2,1...) custom-call(f32[4,640,256]{2,1,0:T(8,128)} %collective-permute-done.1.history_ref), custom_call_target="tpu_custom_call" | custom-call | tf_op jit(solution)/shard_map/split/pallas_call | solution.py:170
  23.1 3.3 %begin.3.refs_8_ = f32[2,4,64,256]{3,2,1,0:T(8,128)} custom-call(f32[64,8,128]{2,1,0:T(8,128)S(1)} %get-tuple-element.37.sigma_ref, bf16[2,640,256]{2,1,0:T(8,128)(2,1)} %get-tuple-element.38.refs_0_, bf16[2,640,256]{2,1,0:T(8,128)(2,1)} %get-tuple-element.39.refs_1_, bf16[2,640,256]{2,1,0:T(8,128)(2,1)} %get-tuple-element.40.refs_2_, ...), custom_call_target="tpu_custom_call" | custom-call | tf_op jit(solution)/shard_map/begin/pallas_call | solution.py:280
  26.5 3.6 %all-to-all-done.sigma_ref = f32[4,64,8,128]{3,2,1,0:T(8,128)S(1)} async-done(((f32[4,64,8,128]{3,2,1,0:T(8,128)}), f32[4,64,8,128]{3,2,1,0:T(8,128)S(1)}, u32[]{:S(2)}, u32[]{:S(2)}) %all-to-all-start) | async-done | bytes 1048608 | tf_op jit(solution)/shard_map/all_to_all | solution.py:487
  30.0 3.1 %shard_map.50 = (f32[2,4,64,256]{3,2,1,0:T(8,128)}, f32[64,8,128]{2,1,0:T(8,128)S(1)}) custom-call(f32[3,2,64,4]{3,2,1,0:T(8,128)S(1)} %copy.10.factor_ref, f32[4,64,8,128]{3,2,1,0:T(8,128)S(1)} %all-to-all-done.sigma_ref, bf16[2,384,256]{2,1,0:T(8,128)(2,1)S(1)} %get-tuple-element.29.refs_0_, bf16[2,384,256]{2,1,0:T(8,128)(2,1)S(1)} %get-tuple-element.30.refs_1_, ...), custom_call_target="tpu_custom_call" | custom-call | tf_op jit(solution)/shard_map/pallas_call | solution.py:394
  33.1 23.5 %all_to_all.45.parts_ref = f32[64,8,128]{2,1,0:T(8,128)S(1)} all-to-all(f32[64,8,128]{2,1,0:T(8,128)S(1)} %get-tuple-element.45), channel_id=1, replica_groups=mesh['mom_0'=8,'mom_1'=8,'core_of_chip'=2,'tm'=4] {'mom_0','mom_1'}, dimensions={0} | all-to-all | bytes 524288 | tf_op jit(solution)/shard_map/all_to_all | solution.py:499
  56.6 18.4 %all_to_all.46.value_ref.sigma_ref = f32[64,8,128]{2,1,0:T(8,128)S(1)} all-to-all(f32[64,8,128]{2,1,0:T(8,128)S(1)} %shard_map.51), channel_id=1, replica_groups=mesh['mom_0'=8,'mom_1'=8,'core_of_chip'=2,'tm'=4] {'mom_0','mom_1'}, dimensions={0} | all-to-all | bytes 524288 | tf_op jit(solution)/shard_map/all_to_all | solution.py:500
  75.0 1.0 copies.2
  76.0 3.5 %all-to-all-start.3 = ((f32[4,64,8,128]{3,2,1,0:T(8,128)}), f32[4,64,8,128]{3,2,1,0:T(8,128)S(1)}, u32[]{:S(2)}, u32[]{:S(2)}) async-start(f32[4,64,8,128]{3,2,1,0:T(8,128)} %copies.2), calls=%async_computation.3 | async-start | bytes 2097152 | tf_op jit(solution)/shard_map/all_to_all | solution.py:504
  79.6 5.4 %collective-permute-start.2 = (f32[2,4,64,256]{3,2,1,0:T(8,128)}, f32[2,4,64,256]{3,2,1,0:T(8,128)}, u32[]{:S(2)}, u32[]{:S(2)}) collective-permute-start(f32[2,4,64,256]{3,2,1,0:T(8,128)} %get-tuple-element.46.refs_8_.refs_9_), channel_id=1, source_target_pairs={{0,4},{4,0},{1,5},{5,1},{2,6},{6,2},{3,7},{7,3},{8,12},{12,8},{9,1... | collective-permute-start | bytes 1572872 | tf_op jit(solution)/shard_map/ppermute | solution.py:484
  84.9 3.3 %begin.4.refs_8_ = f32[2,4,64,256]{3,2,1,0:T(8,128)} custom-call(f32[64,8,128]{2,1,0:T(8,128)S(1)} %all_to_all.46.value_ref.sigma_ref, bf16[2,640,256]{2,1,0:T(8,128)(2,1)} %get-tuple-element.38.refs_0_, bf16[2,640,256]{2,1,0:T(8,128)(2,1)} %get-tuple-element.39.refs_1_, bf16[2,640,256]{2,1,0:T(8,128)(2,1)} %get-tuple-element.40.refs_2_, ...), custom_call_target="tpu_custom_call" | custom-call | tf_op jit(solution)/shard_map/begin/pallas_call | solution.py:280
  88.3 0.0 collective-permute-done.2.refs_10_.refs_11_
  88.3 2.7 %all-to-all-done.3.sigma_ref = f32[4,64,8,128]{3,2,1,0:T(8,128)S(1)} async-done(((f32[4,64,8,128]{3,2,1,0:T(8,128)}), f32[4,64,8,128]{3,2,1,0:T(8,128)S(1)}, u32[]{:S(2)}, u32[]{:S(2)}) %all-to-all-start.3) | async-done | bytes 1048608 | tf_op jit(solution)/shard_map/all_to_all | solution.py:504
  90.9 3.9 %shard_map.52 = (f32[2,4,64,256]{3,2,1,0:T(8,128)}, f32[64,8,128]{2,1,0:T(8,128)S(1)}) custom-call(f32[3,2,64,4]{3,2,1,0:T(8,128)S(1)} %copy.10.factor_ref, f32[4,64,8,128]{3,2,1,0:T(8,128)S(1)} %all-to-all-done.3.sigma_ref, bf16[2,384,256]{2,1,0:T(8,128)(2,1)S(1)} %get-tuple-element.29.refs_0_, bf16[2,384,256]{2,1,0:T(8,128)(2,1)S(1)} %get-tuple-element.30.refs_1_, ...), custom_call_target="tpu_custom_call" | custom-call | tf_op jit(solution)/shard_map/pallas_call | solution.py:394
  94.9 21.2 %all_to_all.47.parts_ref = f32[64,8,128]{2,1,0:T(8,128)S(1)} all-to-all(f32[64,8,128]{2,1,0:T(8,128)S(1)} %get-tuple-element.47), channel_id=1, replica_groups=mesh['mom_0'=8,'mom_1'=8,'core_of_chip'=2,'tm'=4] {'mom_0','mom_1'}, dimensions={0} | all-to-all | bytes 524288 | tf_op jit(solution)/shard_map/all_to_all | solution.py:499
  116.1 17.0 %all_to_all.48.value_ref.sigma_ref = f32[64,8,128]{2,1,0:T(8,128)S(1)} all-to-all(f32[64,8,128]{2,1,0:T(8,128)S(1)} %shard_map.53), channel_id=1, replica_groups=mesh['mom_0'=8,'mom_1'=8,'core_of_chip'=2,'tm'=4] {'mom_0','mom_1'}, dimensions={0} | all-to-all | bytes 524288 | tf_op jit(solution)/shard_map/all_to_all | solution.py:500
  133.1 1.0 copies.3
  134.1 3.5 %all-to-all-start.6 = ((f32[4,64,8,128]{3,2,1,0:T(8,128)}), f32[4,64,8,128]{3,2,1,0:T(8,128)S(1)}, u32[]{:S(2)}, u32[]{:S(2)}) async-start(f32[4,64,8,128]{3,2,1,0:T(8,128)} %copies.3), calls=%async_computation.6 | async-start | bytes 2097152 | tf_op jit(solution)/shard_map/all_to_all | solution.py:504
  137.7 6.0 %collective-permute-start.3 = (f32[2,4,64,256]{3,2,1,0:T(8,128)}, f32[2,4,64,256]{3,2,1,0:T(8,128)}, u32[]{:S(2)}, u32[]{:S(2)}) collective-permute-start(f32[2,4,64,256]{3,2,1,0:T(8,128)} %get-tuple-element.48.refs_8_.refs_10_), channel_id=1, source_target_pairs={{0,4},{4,0},{1,5},{5,1},{2,6},{6,2},{3,7},{7,3},{8,12},{12,8},{9,1... | collective-permute-start | bytes 1572872 | tf_op jit(solution)/shard_map/ppermute | solution.py:484
  143.7 3.3 %begin.5.refs_8_ = f32[2,4,64,256]{3,2,1,0:T(8,128)} custom-call(f32[64,8,128]{2,1,0:T(8,128)S(1)} %all_to_all.48.value_ref.sigma_ref, bf16[2,640,256]{2,1,0:T(8,128)(2,1)} %get-tuple-element.38.refs_0_, bf16[2,640,256]{2,1,0:T(8,128)(2,1)} %get-tuple-element.39.refs_1_, bf16[2,640,256]{2,1,0:T(8,128)(2,1)} %get-tuple-element.40.refs_2_, ...), custom_call_target="tpu_custom_call" | custom-call | tf_op jit(solution)/shard_map/begin/pallas_call | solution.py:280
  147.0 0.0 collective-permute-done.3.refs_12_
  147.0 1.4 all-to-all-done.6.sigma_ref
  148.4 4.6 %shard_map.54 = (f32[4,64,256]{2,1,0:T(8,128)}, f32[4,64,256]{2,1,0:T(8,128)}, f32[64,8,128]{2,1,0:T(8,128)S(1)}) custom-call(f32[3,2,64,4]{3,2,1,0:T(8,128)S(1)} %copy.10.factor_ref, f32[4,64,8,128]{3,2,1,0:T(8,128)S(1)} %all-to-all-done.6.sigma_ref, bf16[2,384,256]{2,1,0:T(8,128)(2,1)S(1)} %get-tuple-element.29.refs_0_, ...), custom_call_target="tpu_custom_call" | custom-call | tf_op jit(solution)/shard_map/pallas_call | solution.py:394
  153.0 17.0 %all_to_all.49.parts_ref = f32[64,8,128]{2,1,0:T(8,128)S(1)} all-to-all(f32[64,8,128]{2,1,0:T(8,128)S(1)} %get-tuple-element.51), channel_id=1, replica_groups=mesh['mom_0'=8,'mom_1'=8,'core_of_chip'=2,'tm'=4] {'mom_0','mom_1'}, dimensions={0} | all-to-all | bytes 524288 | tf_op jit(solution)/shard_map/all_to_all | solution.py:499
  170.0 0.7 shard_map.56
  170.8 4.6 %all-to-all-start.8 = ((f32[64,8,128]{2,1,0:T(8,128)}), f32[64,8,128]{2,1,0:T(8,128)S(1)}, u32[]{:S(2)}, u32[]{:S(2)}) async-start(f32[64,8,128]{2,1,0:T(8,128)} %shard_map.56), calls=%async_computation.8 | async-start | bytes 524288 | tf_op jit(solution)/shard_map/all_to_all | solution.py:500
  175.4 7.9 %collective-permute-start.4 = (f32[4,64,256]{2,1,0:T(8,128)}, f32[4,64,256]{2,1,0:T(8,128)S(1)}, u32[]{:S(2)}, u32[]{:S(2)}) collective-permute-start(f32[4,64,256]{2,1,0:T(8,128)} %get-tuple-element.50), channel_id=1, source_target_pairs={{0,4},{4,0},{1,5},{5,1},{2,6},{6,2},{3,7},{7,3},{8,12},{12,8},{9,1... | collective-permute-start | bytes 786440 | tf_op jit(solution)/shard_map/ppermute | solution.py:484
  183.3 1.4 collective-permute-done.4.theirs_ref
  184.6 0.0 copy-start
  184.6 0.9 copy-done
  185.6 0.8 shard_map.55
  186.4 1.6 all-to-all-done.8.mine_ref
  188.0 8.9 %collective-permute-start.5 = (f32[64,8,128]{2,1,0:T(8,128)S(1)}, f32[64,8,128]{2,1,0:T(8,128)S(1)}, u32[]{:S(2)}, u32[]{:S(2)}) collective-permute-start(f32[64,8,128]{2,1,0:T(8,128)S(1)} %all-to-all-done.8.mine_ref), channel_id=1, source_target_pairs={{0,4},{4,0},{1,5},{5,1},{2,6},{6,2},{3,7},{7,3},{8,12},{12,8},{9,1... | collective-permute-start | bytes 786440 | tf_op jit(solution)/shard_map/ppermute | solution.py:484
  196.9 1.1 collective-permute-done.5.theirs_ref
  198.1 0.8 shard_map.57
  (6 shorter events, 0.2 us)
Async XLA Ops:
  0.6 14.3 %copy-start.1 = (f32[4,1,384]{2,1,0:T(1,128)S(1)}, f32[4,1,384]{2,1,0:T(1,128)}, u32[]{:S(2)}) copy-start(f32[4,1,384]{2,1,0:T(1,128)} %param.5) | copy-start | bytes 18436
  0.6 19.5 %collective-permute-start.1 = (f32[4,640,256]{2,1,0:T(8,128)}, f32[4,640,256]{2,1,0:T(8,128)}, u32[]{:S(2)}, u32[]{:S(2)}) collective-permute-start(f32[4,640,256]{2,1,0:T(8,128)} %bitcast.12), channel_id=1, source_target_pairs={{0,4},{4,0},{1,5},{5,1},{2,6},{6,2},{3,7},{7,3},{8,12},{12,8},{9,1... | collective-permute-start | bytes 7864328 | tf_op jit(solution)/shard_map/ppermute | solution.py:484
  11.4 18.7 %all-to-all-start = ((f32[4,64,8,128]{3,2,1,0:T(8,128)}), f32[4,64,8,128]{3,2,1,0:T(8,128)S(1)}, u32[]{:S(2)}, u32[]{:S(2)}) async-start(f32[4,64,8,128]{3,2,1,0:T(8,128)} %get-tuple-element.28), calls=%async_computation | async-start | bytes 2097152 | tf_op jit(solution)/shard_map/all_to_all | solution.py:487
  14.9 4.9 %collective-permute-start = (f32[4,384]{1,0:T(4,128)S(1)}, f32[4,384]{1,0:T(4,128)S(1)}, u32[]{:S(2)}, u32[]{:S(2)}) collective-permute-start(f32[4,384]{1,0:T(4,128)S(1)} %bitcast.16), channel_id=1, source_target_pairs={{0,4},{4,0},{1,5},{5,1},{2,6},{6,2},{3,7},{7,3},{8,12},{12,8},{9,1... | collective-permute-start | bytes 18440 | tf_op jit(solution)/shard_map/ppermute | solution.py:484
  76.0 14.9 %all-to-all-start.3 = ((f32[4,64,8,128]{3,2,1,0:T(8,128)}), f32[4,64,8,128]{3,2,1,0:T(8,128)S(1)}, u32[]{:S(2)}, u32[]{:S(2)}) async-start(f32[4,64,8,128]{3,2,1,0:T(8,128)} %copies.2), calls=%async_computation.3 | async-start | bytes 2097152 | tf_op jit(solution)/shard_map/all_to_all | solution.py:504
  79.6 8.7 %collective-permute-start.2 = (f32[2,4,64,256]{3,2,1,0:T(8,128)}, f32[2,4,64,256]{3,2,1,0:T(8,128)}, u32[]{:S(2)}, u32[]{:S(2)}) collective-permute-start(f32[2,4,64,256]{3,2,1,0:T(8,128)} %get-tuple-element.46.refs_8_.refs_9_), channel_id=1, source_target_pairs={{0,4},{4,0},{1,5},{5,1},{2,6},{6,2},{3,7},{7,3},{8,12},{12,8},{9,1... | collective-permute-start | bytes 1572872 | tf_op jit(solution)/shard_map/ppermute | solution.py:484
  134.1 14.3 %all-to-all-start.6 = ((f32[4,64,8,128]{3,2,1,0:T(8,128)}), f32[4,64,8,128]{3,2,1,0:T(8,128)S(1)}, u32[]{:S(2)}, u32[]{:S(2)}) async-start(f32[4,64,8,128]{3,2,1,0:T(8,128)} %copies.3), calls=%async_computation.6 | async-start | bytes 2097152 | tf_op jit(solution)/shard_map/all_to_all | solution.py:504
  137.7 9.4 %collective-permute-start.3 = (f32[2,4,64,256]{3,2,1,0:T(8,128)}, f32[2,4,64,256]{3,2,1,0:T(8,128)}, u32[]{:S(2)}, u32[]{:S(2)}) collective-permute-start(f32[2,4,64,256]{3,2,1,0:T(8,128)} %get-tuple-element.48.refs_8_.refs_10_), channel_id=1, source_target_pairs={{0,4},{4,0},{1,5},{5,1},{2,6},{6,2},{3,7},{7,3},{8,12},{12,8},{9,1... | collective-permute-start | bytes 1572872 | tf_op jit(solution)/shard_map/ppermute | solution.py:484
  170.8 17.2 %all-to-all-start.8 = ((f32[64,8,128]{2,1,0:T(8,128)}), f32[64,8,128]{2,1,0:T(8,128)S(1)}, u32[]{:S(2)}, u32[]{:S(2)}) async-start(f32[64,8,128]{2,1,0:T(8,128)} %shard_map.56), calls=%async_computation.8 | async-start | bytes 524288 | tf_op jit(solution)/shard_map/all_to_all | solution.py:500
  175.4 9.2 %collective-permute-start.4 = (f32[4,64,256]{2,1,0:T(8,128)}, f32[4,64,256]{2,1,0:T(8,128)S(1)}, u32[]{:S(2)}, u32[]{:S(2)}) collective-permute-start(f32[4,64,256]{2,1,0:T(8,128)} %get-tuple-element.50), channel_id=1, source_target_pairs={{0,4},{4,0},{1,5},{5,1},{2,6},{6,2},{3,7},{7,3},{8,12},{12,8},{9,1... | collective-permute-start | bytes 786440 | tf_op jit(solution)/shard_map/ppermute | solution.py:484
  184.6 0.9 copy-start
  188.0 10.1 %collective-permute-start.5 = (f32[64,8,128]{2,1,0:T(8,128)S(1)}, f32[64,8,128]{2,1,0:T(8,128)S(1)}, u32[]{:S(2)}, u32[]{:S(2)}) collective-permute-start(f32[64,8,128]{2,1,0:T(8,128)S(1)} %all-to-all-done.8.mine_ref), channel_id=1, source_target_pairs={{0,4},{4,0},{1,5},{5,1},{2,6},{6,2},{3,7},{7,3},{8,12},{12,8},{9,1... | collective-permute-start | bytes 786440 | tf_op jit(solution)/shard_map/ppermute | solution.py:484

commit v3 on v2

--- a/solution.py
+++ b/solution.py
@@ -294,11 +294,15 @@
     )(near(sigma), *[far(value) for value in (*sources, *previous)])
 
 
-def block_kernel(block, windows, known_rows, step_size, factor_ref, sigma_ref, *refs):
+def block_kernel(block, windows, known_rows, whole, step_size, factor_ref, sigma_ref, *refs):
     near_keys, far_keys = part_keys()
     held = dict(zip(near_keys, refs[: len(near_keys)], strict=True))
     refs = refs[len(near_keys) :]
     count = len(far_keys) + 1 + 2 * windows
+    if whole:
+        pair, parts, refs = refs[:2], refs[2:10], refs[10:]
+        *refs, arrived_first, arrived_pair = refs
+        firsts, refs = refs[-8:], refs[:-8]
     sources, outs, buffers = refs[:count], refs[count : -(count + 3)], refs[-(count + 3) : -3]
     arrived, sigma_scratch, joined = refs[-3:]
     piece_ref, outs = outs[-1], outs[:-1]
@@ -319,8 +323,14 @@
             if key[1] == o
         ] + [
             pltpu.make_async_copy(sources[i].at[:, pl.ds(2 * o, 2)], buffers[i].at[:, pl.ds(2 * o, 2)], arrived.at[o, i])
-            for i in range(rows_at, count)
+            for i in range(rows_at + whole, count)
         ])
+        if whole:
+            span = pl.ds(2 * o, 2)
+            for m in range(2):
+                copies[o].append(pltpu.make_async_copy(pair[m].at[span], base_ref.at[m, span], arrived_pair.at[o, m]))
+                for i in (4 * m + 2 * o, 4 * m + 2 * o + 1):
+                    copies[o].append(pltpu.make_async_copy(parts[i].at[:, pl.ds(0, cols)], firsts[i], arrived_first.at[i]))
         for copy in copies[o]:
             copy.start()
     core, here = lax.axis_index(CORE), lax.axis_index("tm")
@@ -331,13 +341,14 @@
 
     for orbital in range(orbitals):
         base = orbital * per_orbital
-        for tile in range(wide, pl.cdiv(used, LANES)):
+        skipped = 0 if whole else cols
+        for tile in range(skipped // LANES, pl.cdiv(used, LANES)):
             start, shard = LANES * tile, tile // wide
             drop = None
-            if start < known_rows:
+            if start < known_rows and not whole:
                 ids = start + lax.broadcasted_iota(jnp.int32, (4 * rows // 2, LANES), 1)
                 drop = jnp.logical_and(here == shard, ids < known_rows)
-            lanes = slice(start - cols, start - cols + LANES)
+            lanes = slice(start - skipped, start - skipped + LANES)
             unpack(lambda i, at=base, j=shard: sigma_ref[j, at + i], sigma_scratch, rows, tile, lanes, wide, drop)
         for copy in copies[orbital]:
             copy.wait()
@@ -347,11 +358,14 @@
             products = []
             for part in range(2):
                 high, low = (held[momentum, orbital, half][part] for half in range(2))
-                total = product(sigma_scratch, rows, slice(0, known_rows - cols), high, low)
+                total = product(sigma_scratch, rows, slice(cols - skipped, known_rows - skipped), high, low)
+                if whole:
+                    high, low = (firsts[4 * momentum + 2 * orbital + half][part] for half in range(2))
+                    total += product(sigma_scratch, rows, slice(0, cols), high, low)
                 for window in range(windows):
                     joined[mine_at, :] = mine_refs[window][momentum, 2 * orbital + part]
                     joined[theirs_at, :] = theirs_refs[window][1 - momentum, 2 * orbital + part]
-                    start = known_rows - cols + window * 2 * rows
+                    start = known_rows - skipped + window * 2 * rows
                     total += product(sigma_scratch, rows, slice(start, start + 2 * rows), *halves_of(joined[...]))
                 products.append(total)
             real, imag = combined(*products, rows)
@@ -382,29 +396,33 @@
 
 
 def advance(block, last, step_size, sigma, factors, known, held, base, mine, theirs):
-    _, comps, rows, cols = base.shape
+    whole = len(base) == 2
+    comps, rows, cols = base[0].shape[-3:]
     known_rows = known[0][0].shape[1]
     used = pl.cdiv(known_rows + len(mine) * 2 * rows, LANES) * LANES
     near_keys, far_keys = part_keys()
     far_parts = [known[m][2 * o + half] for m, o, half in far_keys]
     near_parts = [held[m][2 * o + half] for m, o, half in near_keys]
-    sources = [*far_parts, base, *mine, *theirs]
+    sources = [*far_parts, base[0], *mine, *theirs]
+    extra = [*base, *known[0], *known[1]] if whole else []
     greens = [far_out((comps, rows, cols))] * 2 if last else [far_out((2, comps, rows, cols))]
     vmem = pl.BlockSpec(memory_space=pltpu.VMEM)
     *greens, pieces = pl.pallas_call(
-        functools.partial(block_kernel, block, len(mine), known_rows, step_size),
+        functools.partial(block_kernel, block, len(mine), known_rows, whole, step_size),
         out_shape=(*greens, near_out((sigma.shape[1], 8, LANES))),
-        in_specs=[vmem] * (2 + len(near_keys)) + [pl.BlockSpec(memory_space=pl.ANY)] * len(sources),
+        in_specs=[vmem] * (2 + len(near_keys)) + [pl.BlockSpec(memory_space=pl.ANY)] * (len(sources) + len(extra)),
         out_specs=(vmem,) * (len(greens) + 1),
         scratch_shapes=[
             *[pltpu.VMEM((2, known_rows - cols, cols), jnp.bfloat16)] * len(far_parts),
-            *[pltpu.VMEM(source.shape, source.dtype) for source in sources[len(far_parts) :]],
+            *[pltpu.VMEM((2, comps, rows, cols), jnp.float32)] * (1 + 2 * len(mine)),
             pltpu.SemaphoreType.DMA((comps // 2, len(sources))),
-            pltpu.VMEM((4 * rows, used - cols), jnp.bfloat16),
+            pltpu.VMEM((4 * rows, used if whole else used - cols), jnp.bfloat16),
             pltpu.VMEM((2 * rows, cols), jnp.float32),
+            *([pltpu.VMEM((2, cols, cols), jnp.bfloat16)] * 8 if whole else []),
+            *([pltpu.SemaphoreType.DMA((8,)), pltpu.SemaphoreType.DMA((comps // 2, 2))] if whole else []),
         ],
         compiler_params=pltpu.CompilerParams(vmem_limit_bytes=VMEM_LIMIT),
-    )(factors, near(sigma), *map(near, near_parts), *map(far, sources))
+    )(factors, near(sigma), *map(near, near_parts), *map(far, extra), *map(far, sources))
     return greens, pieces
 
 
@@ -494,7 +512,7 @@
     mine, theirs = [], []
     for block in range(blocks):
         last = block + 1 == blocks
-        base = begin(step_size, sigma_cols, known, greens)
+        base = [begin(step_size, sigma_cols, known, greens)] if block else greens
         greens, pieces = advance(block, last, step_size, sigma, factors, known, held, base, mine, theirs)
         parts = lax.all_to_all(pieces, YZ, 0, 0, tiled=True)
         sigma_cols = lax.all_to_all(cube(parts, norm_factor), YZ, 0, 0, tiled=True)

time: 200 us -> 202 us (1.010)
  waiting for transfers between devices: 11.7 us -> 15 us
    all_to_all x1, waiting for transfers between devices: 3.59 us -> 6.92 us  [body(): sigma = lax.all_to_all(packed_first, 'tm', 0, 0, tiled=True)]
    pallas_call x3 -> x2, Pallas kernels: 9.97 us -> 6.65 us  [begin(): pl.pallas_call(functools.partial(begin_kernel, len(previous) == 1, step_s...]
  transfers between devices with their start and end apart: 10 -> 10, of which waited for: 6 -> 6; matrix products, arithmetic and copies ran while one was open for 0% -> 0% of each run, Pallas kernels for 9% -> 8%
where the time goes in v3:
time: 202 us; the launch traced here: 201 us
  blocking collectives  97 us (48%)
  starting transfers between devices  54.1 us (27%)
  Pallas kernels  32.2 us (16%)
  waiting for transfers between devices  15 us (7%)
    all_to_all x3, blocking collectives, body(): parts = lax.all_to_all(pieces, YZ, 0, 0, tiled=True)  61.6 us
    ppermute x6, starting transfers between devices, swapped(): return lax.ppermute(value, CORE, [(0, 1), (1, 0)])  38.9 us
    all_to_all x2, blocking collectives, body(): sigma_cols = lax.all_to_all(cube(parts, norm_factor), YZ, 0, 0, tiled=True)  35.4 us
    pallas_call x3, Pallas kernels, advance(): pl.pallas_call(functools.partial(block_kernel, block, len(mine), known_ro...  12.5 us
    all_to_all x2, starting transfers between devices, body(): lax.all_to_all(copies_of(sigma_cols, shards), 'tm', 0, 0, tiled=True)  7.05 us
    all_to_all x1, waiting for transfers between devices, body(): sigma = lax.all_to_all(packed_first, 'tm', 0, 0, tiled=True)  6.92 us
    pallas_call x2, Pallas kernels, begin(): pl.pallas_call(functools.partial(begin_kernel, len(previous) == 1, step_s...  6.65 us
    pallas_call x2, Pallas kernels, split(): pl.pallas_call(functools.partial(split_kernel, resident), out_shape=(*[fa...  5.86 us
  transfers between devices with their start and end apart: 10, of which 6 were waited for; matrix products, arithmetic and copies ran while one was open for 0% of the time, Pallas kernels for 8%

profile of v3, /device:TPU:1, one launch (start us, length us, event | category | flops | bytes accessed | tf_op | source)
XLA Modules:
  0.0 200.6 jit_solution(14335461698117066192)
XLA Ops:
  0.6 0.0 copy-start.1
  0.6 8.8 %collective-permute-start.1 = (f32[4,640,256]{2,1,0:T(8,128)}, f32[4,640,256]{2,1,0:T(8,128)}, u32[]{:S(2)}, u32[]{:S(2)}) collective-permute-start(f32[4,640,256]{2,1,0:T(8,128)} %bitcast.12), channel_id=1, source_target_pairs={{0,4},{4,0},{1,5},{5,1},{2,6},{6,2},{3,7},{7,3},{8,12},{12,8},{9,1... | collective-permute-start | bytes 7864328 | tf_op jit(solution)/shard_map/ppermute | solution.py:502
  9.4 2.7 %pack.1 = (f32[4,64,8,128]{3,2,1,0:T(8,128)}, f32[64,8,128]{2,1,0:T(8,128)}) custom-call(f32[4,128,256]{2,1,0:T(8,128)} %sigma_ref.1), custom_call_target="tpu_custom_call" | custom-call | tf_op jit(solution)/shard_map/pack/pallas_call | solution.py:107
  12.1 3.5 %all-to-all-start = ((f32[4,64,8,128]{3,2,1,0:T(8,128)}), f32[4,64,8,128]{3,2,1,0:T(8,128)S(1)}, u32[]{:S(2)}, u32[]{:S(2)}) async-start(f32[4,64,8,128]{3,2,1,0:T(8,128)} %get-tuple-element.27), calls=%async_computation | async-start | bytes 2097152 | tf_op jit(solution)/shard_map/all_to_all | solution.py:505
  15.6 0.0 copy-done.1
  15.6 1.9 collective-permute-start
  17.6 2.9 %split.2 = (bf16[2,640,256]{2,1,0:T(8,128)(2,1)}, bf16[2,640,256]{2,1,0:T(8,128)(2,1)}, bf16[2,640,256]{2,1,0:T(8,128)(2,1)}, bf16[2,640,256]{2,1,0:T(8,128)(2,1...) custom-call(f32[4,640,256]{2,1,0:T(8,128)} %bitcast.13), custom_call_target="tpu_custom_call" | custom-call | tf_op jit(solution)/shard_map/split/pallas_call | solution.py:170
  20.5 0.1 stack.8
  20.5 0.0 collective-permute-done
  20.6 0.1 stack.9
  20.7 0.1 copy.10.factor_ref
  20.8 0.0 collective-permute-done.1.history_ref
  20.8 3.0 %split.3 = (bf16[2,640,256]{2,1,0:T(8,128)(2,1)}, bf16[2,640,256]{2,1,0:T(8,128)(2,1)}, bf16[2,640,256]{2,1,0:T(8,128)(2,1)}, bf16[2,640,256]{2,1,0:T(8,128)(2,1...) custom-call(f32[4,640,256]{2,1,0:T(8,128)} %collective-permute-done.1.history_ref), custom_call_target="tpu_custom_call" | custom-call | tf_op jit(solution)/shard_map/split/pallas_call | solution.py:170
  23.8 6.9 %all-to-all-done.sigma_ref = f32[4,64,8,128]{3,2,1,0:T(8,128)S(1)} async-done(((f32[4,64,8,128]{3,2,1,0:T(8,128)}), f32[4,64,8,128]{3,2,1,0:T(8,128)S(1)}, u32[]{:S(2)}, u32[]{:S(2)}) %all-to-all-start) | async-done | bytes 1048608 | tf_op jit(solution)/shard_map/all_to_all | solution.py:505
  30.8 4.0 %shard_map.50 = (f32[2,4,64,256]{3,2,1,0:T(8,128)}, f32[64,8,128]{2,1,0:T(8,128)S(1)}) custom-call(f32[3,2,64,4]{3,2,1,0:T(8,128)S(1)} %copy.10.factor_ref, f32[4,64,8,128]{3,2,1,0:T(8,128)S(1)} %all-to-all-done.sigma_ref, bf16[2,384,256]{2,1,0:T(8,128)(2,1)S(1)} %get-tuple-element.28.refs_0_, bf16[2,384,256]{2,1,0:T(8,128)(2,1)S(1)} %get-tuple-element.29.refs_1_, ...), custom_call_target="tpu_custom_call" | custom-call | tf_op jit(solution)/shard_map/pallas_call | solution.py:410
  34.7 23.5 %all_to_all.45.parts_ref = f32[64,8,128]{2,1,0:T(8,128)S(1)} all-to-all(f32[64,8,128]{2,1,0:T(8,128)S(1)} %get-tuple-element.43), channel_id=1, replica_groups=mesh['mom_0'=8,'mom_1'=8,'core_of_chip'=2,'tm'=4] {'mom_0','mom_1'}, dimensions={0} | all-to-all | bytes 524288 | tf_op jit(solution)/shard_map/all_to_all | solution.py:517
  58.2 18.4 %all_to_all.46.value_ref.sigma_ref = f32[64,8,128]{2,1,0:T(8,128)S(1)} all-to-all(f32[64,8,128]{2,1,0:T(8,128)S(1)} %shard_map.51), channel_id=1, replica_groups=mesh['mom_0'=8,'mom_1'=8,'core_of_chip'=2,'tm'=4] {'mom_0','mom_1'}, dimensions={0} | all-to-all | bytes 524288 | tf_op jit(solution)/shard_map/all_to_all | solution.py:518
  76.6 1.0 copies.2
  77.7 3.5 %all-to-all-start.3 = ((f32[4,64,8,128]{3,2,1,0:T(8,128)}), f32[4,64,8,128]{3,2,1,0:T(8,128)S(1)}, u32[]{:S(2)}, u32[]{:S(2)}) async-start(f32[4,64,8,128]{3,2,1,0:T(8,128)} %copies.2), calls=%async_computation.3 | async-start | bytes 2097152 | tf_op jit(solution)/shard_map/all_to_all | solution.py:522
  81.2 5.4 %collective-permute-start.2 = (f32[2,4,64,256]{3,2,1,0:T(8,128)}, f32[2,4,64,256]{3,2,1,0:T(8,128)}, u32[]{:S(2)}, u32[]{:S(2)}) collective-permute-start(f32[2,4,64,256]{3,2,1,0:T(8,128)} %get-tuple-element.44.refs_8_.refs_9_), channel_id=1, source_target_pairs={{0,4},{4,0},{1,5},{5,1},{2,6},{6,2},{3,7},{7,3},{8,12},{12,8},{9,1... | collective-permute-start | bytes 1572872 | tf_op jit(solution)/shard_map/ppermute | solution.py:502
  86.6 3.3 %begin.2.refs_8_ = f32[2,4,64,256]{3,2,1,0:T(8,128)} custom-call(f32[64,8,128]{2,1,0:T(8,128)S(1)} %all_to_all.46.value_ref.sigma_ref, bf16[2,640,256]{2,1,0:T(8,128)(2,1)} %get-tuple-element.35.refs_7_.refs_0_, bf16[2,640,256]{2,1,0:T(8,128)(2,1)} %get-tuple-element.36.refs_8_.refs_1_, bf16[2,640,256]{2,1,0:T(8,128)(2,1)} %get-tuple-element.37.refs_9_.refs_2_, ...), custom_call_target="tpu_custom_call" | custom-call | tf_op jit(solution)/shard_map/begin/pallas_call | solution.py:280
  89.9 0.0 collective-permute-done.2.refs_10_.refs_11_
  89.9 2.7 %all-to-all-done.3.sigma_ref = f32[4,64,8,128]{3,2,1,0:T(8,128)S(1)} async-done(((f32[4,64,8,128]{3,2,1,0:T(8,128)}), f32[4,64,8,128]{3,2,1,0:T(8,128)S(1)}, u32[]{:S(2)}, u32[]{:S(2)}) %all-to-all-start.3) | async-done | bytes 1048608 | tf_op jit(solution)/shard_map/all_to_all | solution.py:522
  92.6 3.9 %shard_map.52 = (f32[2,4,64,256]{3,2,1,0:T(8,128)}, f32[64,8,128]{2,1,0:T(8,128)S(1)}) custom-call(f32[3,2,64,4]{3,2,1,0:T(8,128)S(1)} %copy.10.factor_ref, f32[4,64,8,128]{3,2,1,0:T(8,128)S(1)} %all-to-all-done.3.sigma_ref, bf16[2,384,256]{2,1,0:T(8,128)(2,1)S(1)} %get-tuple-element.28.refs_0_, bf16[2,384,256]{2,1,0:T(8,128)(2,1)S(1)} %get-tuple-element.29.refs_1_, ...), custom_call_target="tpu_custom_call" | custom-call | tf_op jit(solution)/shard_map/pallas_call | solution.py:410
  96.5 21.2 %all_to_all.47.parts_ref = f32[64,8,128]{2,1,0:T(8,128)S(1)} all-to-all(f32[64,8,128]{2,1,0:T(8,128)S(1)} %get-tuple-element.45), channel_id=1, replica_groups=mesh['mom_0'=8,'mom_1'=8,'core_of_chip'=2,'tm'=4] {'mom_0','mom_1'}, dimensions={0} | all-to-all | bytes 524288 | tf_op jit(solution)/shard_map/all_to_all | solution.py:517
  117.7 17.0 %all_to_all.48.value_ref.sigma_ref = f32[64,8,128]{2,1,0:T(8,128)S(1)} all-to-all(f32[64,8,128]{2,1,0:T(8,128)S(1)} %shard_map.53), channel_id=1, replica_groups=mesh['mom_0'=8,'mom_1'=8,'core_of_chip'=2,'tm'=4] {'mom_0','mom_1'}, dimensions={0} | all-to-all | bytes 524288 | tf_op jit(solution)/shard_map/all_to_all | solution.py:518
  134.8 1.0 copies.3
  135.8 3.5 %all-to-all-start.6 = ((f32[4,64,8,128]{3,2,1,0:T(8,128)}), f32[4,64,8,128]{3,2,1,0:T(8,128)S(1)}, u32[]{:S(2)}, u32[]{:S(2)}) async-start(f32[4,64,8,128]{3,2,1,0:T(8,128)} %copies.3), calls=%async_computation.6 | async-start | bytes 2097152 | tf_op jit(solution)/shard_map/all_to_all | solution.py:522
  139.3 6.0 %collective-permute-start.3 = (f32[2,4,64,256]{3,2,1,0:T(8,128)}, f32[2,4,64,256]{3,2,1,0:T(8,128)}, u32[]{:S(2)}, u32[]{:S(2)}) collective-permute-start(f32[2,4,64,256]{3,2,1,0:T(8,128)} %get-tuple-element.46.refs_8_.refs_10_), channel_id=1, source_target_pairs={{0,4},{4,0},{1,5},{5,1},{2,6},{6,2},{3,7},{7,3},{8,12},{12,8},{9,1... | collective-permute-start | bytes 1572872 | tf_op jit(solution)/shard_map/ppermute | solution.py:502
  145.3 3.3 %begin.3.refs_8_ = f32[2,4,64,256]{3,2,1,0:T(8,128)} custom-call(f32[64,8,128]{2,1,0:T(8,128)S(1)} %all_to_all.48.value_ref.sigma_ref, bf16[2,640,256]{2,1,0:T(8,128)(2,1)} %get-tuple-element.35.refs_7_.refs_0_, bf16[2,640,256]{2,1,0:T(8,128)(2,1)} %get-tuple-element.36.refs_8_.refs_1_, bf16[2,640,256]{2,1,0:T(8,128)(2,1)} %get-tuple-element.37.refs_9_.refs_2_, ...), custom_call_target="tpu_custom_call" | custom-call | tf_op jit(solution)/shard_map/begin/pallas_call | solution.py:280
  148.7 0.0 collective-permute-done.3.refs_12_
  148.7 1.4 all-to-all-done.6.sigma_ref
  150.1 4.6 %shard_map.54 = (f32[4,64,256]{2,1,0:T(8,128)}, f32[4,64,256]{2,1,0:T(8,128)}, f32[64,8,128]{2,1,0:T(8,128)S(1)}) custom-call(f32[3,2,64,4]{3,2,1,0:T(8,128)S(1)} %copy.10.factor_ref, f32[4,64,8,128]{3,2,1,0:T(8,128)S(1)} %all-to-all-done.6.sigma_ref, bf16[2,384,256]{2,1,0:T(8,128)(2,1)S(1)} %get-tuple-element.28.refs_0_, ...), custom_call_target="tpu_custom_call" | custom-call | tf_op jit(solution)/shard_map/pallas_call | solution.py:410
  154.7 17.0 %all_to_all.49.parts_ref = f32[64,8,128]{2,1,0:T(8,128)S(1)} all-to-all(f32[64,8,128]{2,1,0:T(8,128)S(1)} %get-tuple-element.49), channel_id=1, replica_groups=mesh['mom_0'=8,'mom_1'=8,'core_of_chip'=2,'tm'=4] {'mom_0','mom_1'}, dimensions={0} | all-to-all | bytes 524288 | tf_op jit(solution)/shard_map/all_to_all | solution.py:517
  171.6 0.7 shard_map.56
  172.4 4.6 %all-to-all-start.8 = ((f32[64,8,128]{2,1,0:T(8,128)}), f32[64,8,128]{2,1,0:T(8,128)S(1)}, u32[]{:S(2)}, u32[]{:S(2)}) async-start(f32[64,8,128]{2,1,0:T(8,128)} %shard_map.56), calls=%async_computation.8 | async-start | bytes 524288 | tf_op jit(solution)/shard_map/all_to_all | solution.py:518
  177.0 7.9 %collective-permute-start.4 = (f32[4,64,256]{2,1,0:T(8,128)}, f32[4,64,256]{2,1,0:T(8,128)S(1)}, u32[]{:S(2)}, u32[]{:S(2)}) collective-permute-start(f32[4,64,256]{2,1,0:T(8,128)} %get-tuple-element.48), channel_id=1, source_target_pairs={{0,4},{4,0},{1,5},{5,1},{2,6},{6,2},{3,7},{7,3},{8,12},{12,8},{9,1... | collective-permute-start | bytes 786440 | tf_op jit(solution)/shard_map/ppermute | solution.py:502
  184.9 1.4 collective-permute-done.4.theirs_ref
  186.3 0.0 copy-start
  186.3 0.9 copy-done
  187.2 0.8 shard_map.55
  188.1 1.6 all-to-all-done.8.mine_ref
  189.6 8.9 %collective-permute-start.5 = (f32[64,8,128]{2,1,0:T(8,128)S(1)}, f32[64,8,128]{2,1,0:T(8,128)S(1)}, u32[]{:S(2)}, u32[]{:S(2)}) collective-permute-start(f32[64,8,128]{2,1,0:T(8,128)S(1)} %all-to-all-done.8.mine_ref), channel_id=1, source_target_pairs={{0,4},{4,0},{1,5},{5,1},{2,6},{6,2},{3,7},{7,3},{8,12},{12,8},{9,1... | collective-permute-start | bytes 786440 | tf_op jit(solution)/shard_map/ppermute | solution.py:502
  198.6 1.1 collective-permute-done.5.theirs_ref
  199.7 0.8 shard_map.57
  (6 shorter events, 0.2 us)
Async XLA Ops:
  0.6 15.0 %copy-start.1 = (f32[4,1,384]{2,1,0:T(1,128)S(1)}, f32[4,1,384]{2,1,0:T(1,128)}, u32[]{:S(2)}) copy-start(f32[4,1,384]{2,1,0:T(1,128)} %param.5) | copy-start | bytes 18436
  0.6 20.2 %collective-permute-start.1 = (f32[4,640,256]{2,1,0:T(8,128)}, f32[4,640,256]{2,1,0:T(8,128)}, u32[]{:S(2)}, u32[]{:S(2)}) collective-permute-start(f32[4,640,256]{2,1,0:T(8,128)} %bitcast.12), channel_id=1, source_target_pairs={{0,4},{4,0},{1,5},{5,1},{2,6},{6,2},{3,7},{7,3},{8,12},{12,8},{9,1... | collective-permute-start | bytes 7864328 | tf_op jit(solution)/shard_map/ppermute | solution.py:502
  12.1 18.7 %all-to-all-start = ((f32[4,64,8,128]{3,2,1,0:T(8,128)}), f32[4,64,8,128]{3,2,1,0:T(8,128)S(1)}, u32[]{:S(2)}, u32[]{:S(2)}) async-start(f32[4,64,8,128]{3,2,1,0:T(8,128)} %get-tuple-element.27), calls=%async_computation | async-start | bytes 2097152 | tf_op jit(solution)/shard_map/all_to_all | solution.py:505
  15.6 4.9 %collective-permute-start = (f32[4,384]{1,0:T(4,128)S(1)}, f32[4,384]{1,0:T(4,128)S(1)}, u32[]{:S(2)}, u32[]{:S(2)}) collective-permute-start(f32[4,384]{1,0:T(4,128)S(1)} %bitcast.16), channel_id=1, source_target_pairs={{0,4},{4,0},{1,5},{5,1},{2,6},{6,2},{3,7},{7,3},{8,12},{12,8},{9,1... | collective-permute-start | bytes 18440 | tf_op jit(solution)/shard_map/ppermute | solution.py:502
  77.7 14.9 %all-to-all-start.3 = ((f32[4,64,8,128]{3,2,1,0:T(8,128)}), f32[4,64,8,128]{3,2,1,0:T(8,128)S(1)}, u32[]{:S(2)}, u32[]{:S(2)}) async-start(f32[4,64,8,128]{3,2,1,0:T(8,128)} %copies.2), calls=%async_computation.3 | async-start | bytes 2097152 | tf_op jit(solution)/shard_map/all_to_all | solution.py:522
  81.2 8.7 %collective-permute-start.2 = (f32[2,4,64,256]{3,2,1,0:T(8,128)}, f32[2,4,64,256]{3,2,1,0:T(8,128)}, u32[]{:S(2)}, u32[]{:S(2)}) collective-permute-start(f32[2,4,64,256]{3,2,1,0:T(8,128)} %get-tuple-element.44.refs_8_.refs_9_), channel_id=1, source_target_pairs={{0,4},{4,0},{1,5},{5,1},{2,6},{6,2},{3,7},{7,3},{8,12},{12,8},{9,1... | collective-permute-start | bytes 1572872 | tf_op jit(solution)/shard_map/ppermute | solution.py:502
  135.8 14.3 %all-to-all-start.6 = ((f32[4,64,8,128]{3,2,1,0:T(8,128)}), f32[4,64,8,128]{3,2,1,0:T(8,128)S(1)}, u32[]{:S(2)}, u32[]{:S(2)}) async-start(f32[4,64,8,128]{3,2,1,0:T(8,128)} %copies.3), calls=%async_computation.6 | async-start | bytes 2097152 | tf_op jit(solution)/shard_map/all_to_all | solution.py:522
  139.3 9.4 %collective-permute-start.3 = (f32[2,4,64,256]{3,2,1,0:T(8,128)}, f32[2,4,64,256]{3,2,1,0:T(8,128)}, u32[]{:S(2)}, u32[]{:S(2)}) collective-permute-start(f32[2,4,64,256]{3,2,1,0:T(8,128)} %get-tuple-element.46.refs_8_.refs_10_), channel_id=1, source_target_pairs={{0,4},{4,0},{1,5},{5,1},{2,6},{6,2},{3,7},{7,3},{8,12},{12,8},{9,1... | collective-permute-start | bytes 1572872 | tf_op jit(solution)/shard_map/ppermute | solution.py:502
  172.4 17.2 %all-to-all-start.8 = ((f32[64,8,128]{2,1,0:T(8,128)}), f32[64,8,128]{2,1,0:T(8,128)S(1)}, u32[]{:S(2)}, u32[]{:S(2)}) async-start(f32[64,8,128]{2,1,0:T(8,128)} %shard_map.56), calls=%async_computation.8 | async-start | bytes 524288 | tf_op jit(solution)/shard_map/all_to_all | solution.py:518
  177.0 9.2 %collective-permute-start.4 = (f32[4,64,256]{2,1,0:T(8,128)}, f32[4,64,256]{2,1,0:T(8,128)S(1)}, u32[]{:S(2)}, u32[]{:S(2)}) collective-permute-start(f32[4,64,256]{2,1,0:T(8,128)} %get-tuple-element.48), channel_id=1, source_target_pairs={{0,4},{4,0},{1,5},{5,1},{2,6},{6,2},{3,7},{7,3},{8,12},{12,8},{9,1... | collective-permute-start | bytes 786440 | tf_op jit(solution)/shard_map/ppermute | solution.py:502
  186.3 0.9 copy-start
  189.6 10.1 %collective-permute-start.5 = (f32[64,8,128]{2,1,0:T(8,128)S(1)}, f32[64,8,128]{2,1,0:T(8,128)S(1)}, u32[]{:S(2)}, u32[]{:S(2)}) collective-permute-start(f32[64,8,128]{2,1,0:T(8,128)S(1)} %all-to-all-done.8.mine_ref), channel_id=1, source_target_pairs={{0,4},{4,0},{1,5},{5,1},{2,6},{6,2},{3,7},{7,3},{8,12},{12,8},{9,1... | collective-permute-start | bytes 786440 | tf_op jit(solution)/shard_map/ppermute | solution.py:502

commit v4 on v3

--- a/solution.py
+++ b/solution.py
@@ -77,7 +77,7 @@
     return copies
 
 
-def pack_kernel(sigma_ref, out_ref, piece_buffer, rows_buffer, arrived, sent):
+def pack_kernel(sigma_ref, out_ref, rows_buffer, piece_buffer, arrived, sent):
     comps, rows = rows_buffer.shape[:2]
     per_orbital = piece_buffer.shape[0] // (comps // 2)
     mine = pl.ds(pl.multiple_of(lax.axis_index(CORE) * rows, 8), rows)
@@ -106,11 +106,12 @@
     anywhere = pl.BlockSpec(memory_space=pl.ANY)
     return pl.pallas_call(
         pack_kernel,
-        out_shape=(far_out((copies, pieces, 8, LANES)), near_out((pieces, 8, LANES))),
+        out_shape=far_out((copies, pieces, 8, LANES)),
         in_specs=[anywhere],
-        out_specs=(anywhere, pl.BlockSpec(memory_space=pltpu.VMEM)),
+        out_specs=anywhere,
         scratch_shapes=[
             pltpu.VMEM((comps, rows // 2, cols), jnp.float32),
+            pltpu.VMEM((pieces, 8, LANES), jnp.float32),
             pltpu.SemaphoreType.DMA((comps // 2,)),
             pltpu.SemaphoreType.DMA((comps // 2, copies)),
         ],
@@ -501,7 +502,7 @@
     def swapped(value):
         return lax.ppermute(value, CORE, [(0, 1), (1, 0)])
 
-    packed_first, sigma_cols = pack(sigma_first, shards)
+    packed_first, sigma_cols = pack(sigma_first, shards), None
     sigma = lax.all_to_all(packed_first, "tm", 0, 0, tiled=True)
     their_history = swapped(history)
     their_propagator = swapped(propagator)

time: 202 us -> 201 us (level)
  no operation moved by 1% of the time
where the time goes in v4:
time: 201 us; the launch traced here: 200 us
  blocking collectives  97.1 us (48%)
  starting transfers between devices  53.5 us (27%)
  Pallas kernels  31.5 us (16%)
  waiting for transfers between devices  15.5 us (8%)
    all_to_all x3, blocking collectives, body(): parts = lax.all_to_all(pieces, YZ, 0, 0, tiled=True)  61.7 us
    ppermute x6, starting transfers between devices, swapped(): return lax.ppermute(value, CORE, [(0, 1), (1, 0)])  38.3 us
    all_to_all x2, blocking collectives, body(): sigma_cols = lax.all_to_all(cube(parts, norm_factor), YZ, 0, 0, tiled=True)  35.4 us
    pallas_call x3, Pallas kernels, advance(): pl.pallas_call(functools.partial(block_kernel, block, len(mine), known_ro...  12.5 us
    all_to_all x2, starting transfers between devices, body(): lax.all_to_all(copies_of(sigma_cols, shards), 'tm', 0, 0, tiled=True)  7.05 us
    all_to_all x1, waiting for transfers between devices, body(): sigma = lax.all_to_all(packed_first, 'tm', 0, 0, tiled=True)  6.91 us
    pallas_call x2, Pallas kernels, begin(): pl.pallas_call(functools.partial(begin_kernel, len(previous) == 1, step_s...  6.64 us
    pallas_call x2, Pallas kernels, split(): pl.pallas_call(functools.partial(split_kernel, resident), out_shape=(*[fa...  5.86 us
  transfers between devices with their start and end apart: 10, of which 6 were waited for; matrix products, arithmetic and copies ran while one was open for 0% of the time, Pallas kernels for 8%

profile of v4, /device:TPU:1, one launch (start us, length us, event | category | flops | bytes accessed | tf_op | source)
XLA Modules:
  0.0 199.9 jit_solution(8155103582556089217)
XLA Ops:
  0.6 0.0 copy-start.1
  0.6 8.8 %collective-permute-start.1 = (f32[4,640,256]{2,1,0:T(8,128)}, f32[4,640,256]{2,1,0:T(8,128)}, u32[]{:S(2)}, u32[]{:S(2)}) collective-permute-start(f32[4,640,256]{2,1,0:T(8,128)} %bitcast.12), channel_id=1, source_target_pairs={{0,4},{4,0},{1,5},{5,1},{2,6},{6,2},{3,7},{7,3},{8,12},{12,8},{9,1... | collective-permute-start | bytes 7864328 | tf_op jit(solution)/shard_map/ppermute | solution.py:503
  9.4 2.0 pack.1
  11.4 3.5 %all-to-all-start = ((f32[4,64,8,128]{3,2,1,0:T(8,128)}), f32[4,64,8,128]{3,2,1,0:T(8,128)S(1)}, u32[]{:S(2)}, u32[]{:S(2)}) async-start(f32[4,64,8,128]{3,2,1,0:T(8,128)} %pack.1), calls=%async_computation | async-start | bytes 2097152 | tf_op jit(solution)/shard_map/all_to_all | solution.py:506
  14.9 0.0 copy-done.1
  14.9 1.9 collective-permute-start
  16.9 2.9 %split.2 = (bf16[2,640,256]{2,1,0:T(8,128)(2,1)}, bf16[2,640,256]{2,1,0:T(8,128)(2,1)}, bf16[2,640,256]{2,1,0:T(8,128)(2,1)}, bf16[2,640,256]{2,1,0:T(8,128)(2,1...) custom-call(f32[4,640,256]{2,1,0:T(8,128)} %bitcast.13), custom_call_target="tpu_custom_call" | custom-call | tf_op jit(solution)/shard_map/split/pallas_call | solution.py:171
  19.8 0.1 stack.8
  19.9 0.0 collective-permute-done
  19.9 0.1 stack.9
  20.0 0.1 copy.10.factor_ref
  20.1 0.0 collective-permute-done.1.history_ref
  20.1 3.0 %split.3 = (bf16[2,640,256]{2,1,0:T(8,128)(2,1)}, bf16[2,640,256]{2,1,0:T(8,128)(2,1)}, bf16[2,640,256]{2,1,0:T(8,128)(2,1)}, bf16[2,640,256]{2,1,0:T(8,128)(2,1...) custom-call(f32[4,640,256]{2,1,0:T(8,128)} %collective-permute-done.1.history_ref), custom_call_target="tpu_custom_call" | custom-call | tf_op jit(solution)/shard_map/split/pallas_call | solution.py:171
  23.1 6.9 %all-to-all-done.sigma_ref = f32[4,64,8,128]{3,2,1,0:T(8,128)S(1)} async-done(((f32[4,64,8,128]{3,2,1,0:T(8,128)}), f32[4,64,8,128]{3,2,1,0:T(8,128)S(1)}, u32[]{:S(2)}, u32[]{:S(2)}) %all-to-all-start) | async-done | bytes 1048608 | tf_op jit(solution)/shard_map/all_to_all | solution.py:506
  30.1 4.0 %shard_map.50 = (f32[2,4,64,256]{3,2,1,0:T(8,128)}, f32[64,8,128]{2,1,0:T(8,128)S(1)}) custom-call(f32[3,2,64,4]{3,2,1,0:T(8,128)S(1)} %copy.10.factor_ref, f32[4,64,8,128]{3,2,1,0:T(8,128)S(1)} %all-to-all-done.sigma_ref, bf16[2,384,256]{2,1,0:T(8,128)(2,1)S(1)} %get-tuple-element.26.refs_0_, bf16[2,384,256]{2,1,0:T(8,128)(2,1)S(1)} %get-tuple-element.27.refs_1_, ...), custom_call_target="tpu_custom_call" | custom-call | tf_op jit(solution)/shard_map/pallas_call | solution.py:411
  34.0 23.4 %all_to_all.45.parts_ref = f32[64,8,128]{2,1,0:T(8,128)S(1)} all-to-all(f32[64,8,128]{2,1,0:T(8,128)S(1)} %get-tuple-element.41), channel_id=1, replica_groups=mesh['mom_0'=8,'mom_1'=8,'core_of_chip'=2,'tm'=4] {'mom_0','mom_1'}, dimensions={0} | all-to-all | bytes 524288 | tf_op jit(solution)/shard_map/all_to_all | solution.py:518
  57.5 18.4 %all_to_all.46.value_ref.sigma_ref = f32[64,8,128]{2,1,0:T(8,128)S(1)} all-to-all(f32[64,8,128]{2,1,0:T(8,128)S(1)} %shard_map.51), channel_id=1, replica_groups=mesh['mom_0'=8,'mom_1'=8,'core_of_chip'=2,'tm'=4] {'mom_0','mom_1'}, dimensions={0} | all-to-all | bytes 524288 | tf_op jit(solution)/shard_map/all_to_all | solution.py:519
  75.9 1.0 copies.2
  77.0 3.5 %all-to-all-start.3 = ((f32[4,64,8,128]{3,2,1,0:T(8,128)}), f32[4,64,8,128]{3,2,1,0:T(8,128)S(1)}, u32[]{:S(2)}, u32[]{:S(2)}) async-start(f32[4,64,8,128]{3,2,1,0:T(8,128)} %copies.2), calls=%async_computation.3 | async-start | bytes 2097152 | tf_op jit(solution)/shard_map/all_to_all | solution.py:523
  80.5 5.4 %collective-permute-start.2 = (f32[2,4,64,256]{3,2,1,0:T(8,128)}, f32[2,4,64,256]{3,2,1,0:T(8,128)}, u32[]{:S(2)}, u32[]{:S(2)}) collective-permute-start(f32[2,4,64,256]{3,2,1,0:T(8,128)} %get-tuple-element.42.refs_8_.refs_9_), channel_id=1, source_target_pairs={{0,4},{4,0},{1,5},{5,1},{2,6},{6,2},{3,7},{7,3},{8,12},{12,8},{9,1... | collective-permute-start | bytes 1572872 | tf_op jit(solution)/shard_map/ppermute | solution.py:503
  85.9 3.3 %begin.2.refs_8_ = f32[2,4,64,256]{3,2,1,0:T(8,128)} custom-call(f32[64,8,128]{2,1,0:T(8,128)S(1)} %all_to_all.46.value_ref.sigma_ref, bf16[2,640,256]{2,1,0:T(8,128)(2,1)} %get-tuple-element.33.refs_7_.refs_0_, bf16[2,640,256]{2,1,0:T(8,128)(2,1)} %get-tuple-element.34.refs_8_.refs_1_, bf16[2,640,256]{2,1,0:T(8,128)(2,1)} %get-tuple-element.35.refs_9_.refs_2_, ...), custom_call_target="tpu_custom_call" | custom-call | tf_op jit(solution)/shard_map/begin/pallas_call | solution.py:281
  89.2 0.0 collective-permute-done.2.refs_10_.refs_11_
  89.2 2.7 %all-to-all-done.3.sigma_ref = f32[4,64,8,128]{3,2,1,0:T(8,128)S(1)} async-done(((f32[4,64,8,128]{3,2,1,0:T(8,128)}), f32[4,64,8,128]{3,2,1,0:T(8,128)S(1)}, u32[]{:S(2)}, u32[]{:S(2)}) %all-to-all-start.3) | async-done | bytes 1048608 | tf_op jit(solution)/shard_map/all_to_all | solution.py:523
  91.9 3.9 %shard_map.52 = (f32[2,4,64,256]{3,2,1,0:T(8,128)}, f32[64,8,128]{2,1,0:T(8,128)S(1)}) custom-call(f32[3,2,64,4]{3,2,1,0:T(8,128)S(1)} %copy.10.factor_ref, f32[4,64,8,128]{3,2,1,0:T(8,128)S(1)} %all-to-all-done.3.sigma_ref, bf16[2,384,256]{2,1,0:T(8,128)(2,1)S(1)} %get-tuple-element.26.refs_0_, bf16[2,384,256]{2,1,0:T(8,128)(2,1)S(1)} %get-tuple-element.27.refs_1_, ...), custom_call_target="tpu_custom_call" | custom-call | tf_op jit(solution)/shard_map/pallas_call | solution.py:411
  95.8 21.2 %all_to_all.47.parts_ref = f32[64,8,128]{2,1,0:T(8,128)S(1)} all-to-all(f32[64,8,128]{2,1,0:T(8,128)S(1)} %get-tuple-element.43), channel_id=1, replica_groups=mesh['mom_0'=8,'mom_1'=8,'core_of_chip'=2,'tm'=4] {'mom_0','mom_1'}, dimensions={0} | all-to-all | bytes 524288 | tf_op jit(solution)/shard_map/all_to_all | solution.py:518
  117.0 17.0 %all_to_all.48.value_ref.sigma_ref = f32[64,8,128]{2,1,0:T(8,128)S(1)} all-to-all(f32[64,8,128]{2,1,0:T(8,128)S(1)} %shard_map.53), channel_id=1, replica_groups=mesh['mom_0'=8,'mom_1'=8,'core_of_chip'=2,'tm'=4] {'mom_0','mom_1'}, dimensions={0} | all-to-all | bytes 524288 | tf_op jit(solution)/shard_map/all_to_all | solution.py:519
  134.1 1.0 copies.3
  135.1 3.5 %all-to-all-start.6 = ((f32[4,64,8,128]{3,2,1,0:T(8,128)}), f32[4,64,8,128]{3,2,1,0:T(8,128)S(1)}, u32[]{:S(2)}, u32[]{:S(2)}) async-start(f32[4,64,8,128]{3,2,1,0:T(8,128)} %copies.3), calls=%async_computation.6 | async-start | bytes 2097152 | tf_op jit(solution)/shard_map/all_to_all | solution.py:523
  138.6 5.9 %collective-permute-start.3 = (f32[2,4,64,256]{3,2,1,0:T(8,128)}, f32[2,4,64,256]{3,2,1,0:T(8,128)}, u32[]{:S(2)}, u32[]{:S(2)}) collective-permute-start(f32[2,4,64,256]{3,2,1,0:T(8,128)} %get-tuple-element.44.refs_8_.refs_10_), channel_id=1, source_target_pairs={{0,4},{4,0},{1,5},{5,1},{2,6},{6,2},{3,7},{7,3},{8,12},{12,8},{9,1... | collective-permute-start | bytes 1572872 | tf_op jit(solution)/shard_map/ppermute | solution.py:503
  144.5 3.3 %begin.3.refs_8_ = f32[2,4,64,256]{3,2,1,0:T(8,128)} custom-call(f32[64,8,128]{2,1,0:T(8,128)S(1)} %all_to_all.48.value_ref.sigma_ref, bf16[2,640,256]{2,1,0:T(8,128)(2,1)} %get-tuple-element.33.refs_7_.refs_0_, bf16[2,640,256]{2,1,0:T(8,128)(2,1)} %get-tuple-element.34.refs_8_.refs_1_, bf16[2,640,256]{2,1,0:T(8,128)(2,1)} %get-tuple-element.35.refs_9_.refs_2_, ...), custom_call_target="tpu_custom_call" | custom-call | tf_op jit(solution)/shard_map/begin/pallas_call | solution.py:281
  147.8 0.0 collective-permute-done.3.refs_12_
  147.8 1.7 all-to-all-done.6.sigma_ref
  149.5 4.6 %shard_map.54 = (f32[4,64,256]{2,1,0:T(8,128)}, f32[4,64,256]{2,1,0:T(8,128)}, f32[64,8,128]{2,1,0:T(8,128)S(1)}) custom-call(f32[3,2,64,4]{3,2,1,0:T(8,128)S(1)} %copy.10.factor_ref, f32[4,64,8,128]{3,2,1,0:T(8,128)S(1)} %all-to-all-done.6.sigma_ref, bf16[2,384,256]{2,1,0:T(8,128)(2,1)S(1)} %get-tuple-element.26.refs_0_, ...), custom_call_target="tpu_custom_call" | custom-call | tf_op jit(solution)/shard_map/pallas_call | solution.py:411
  154.2 17.0 %all_to_all.49.parts_ref = f32[64,8,128]{2,1,0:T(8,128)S(1)} all-to-all(f32[64,8,128]{2,1,0:T(8,128)S(1)} %get-tuple-element.47), channel_id=1, replica_groups=mesh['mom_0'=8,'mom_1'=8,'core_of_chip'=2,'tm'=4] {'mom_0','mom_1'}, dimensions={0} | all-to-all | bytes 524288 | tf_op jit(solution)/shard_map/all_to_all | solution.py:518
  171.2 0.7 shard_map.56
  171.9 4.6 %all-to-all-start.8 = ((f32[64,8,128]{2,1,0:T(8,128)}), f32[64,8,128]{2,1,0:T(8,128)S(1)}, u32[]{:S(2)}, u32[]{:S(2)}) async-start(f32[64,8,128]{2,1,0:T(8,128)} %shard_map.56), calls=%async_computation.8 | async-start | bytes 524288 | tf_op jit(solution)/shard_map/all_to_all | solution.py:519
  176.5 7.7 %collective-permute-start.4 = (f32[4,64,256]{2,1,0:T(8,128)}, f32[4,64,256]{2,1,0:T(8,128)S(1)}, u32[]{:S(2)}, u32[]{:S(2)}) collective-permute-start(f32[4,64,256]{2,1,0:T(8,128)} %get-tuple-element.46), channel_id=1, source_target_pairs={{0,4},{4,0},{1,5},{5,1},{2,6},{6,2},{3,7},{7,3},{8,12},{12,8},{9,1... | collective-permute-start | bytes 786440 | tf_op jit(solution)/shard_map/ppermute | solution.py:503
  184.2 1.4 collective-permute-done.4.theirs_ref
  185.6 0.0 copy-start
  185.6 0.9 copy-done
  186.5 0.8 shard_map.55
  187.4 1.7 all-to-all-done.8.mine_ref
  189.1 8.8 %collective-permute-start.5 = (f32[64,8,128]{2,1,0:T(8,128)S(1)}, f32[64,8,128]{2,1,0:T(8,128)S(1)}, u32[]{:S(2)}, u32[]{:S(2)}) collective-permute-start(f32[64,8,128]{2,1,0:T(8,128)S(1)} %all-to-all-done.8.mine_ref), channel_id=1, source_target_pairs={{0,4},{4,0},{1,5},{5,1},{2,6},{6,2},{3,7},{7,3},{8,12},{12,8},{9,1... | collective-permute-start | bytes 786440 | tf_op jit(solution)/shard_map/ppermute | solution.py:503
  197.9 1.1 collective-permute-done.5.theirs_ref
  199.0 0.8 shard_map.57
  (6 shorter events, 0.2 us)
Async XLA Ops:
  0.6 14.3 %copy-start.1 = (f32[4,1,384]{2,1,0:T(1,128)S(1)}, f32[4,1,384]{2,1,0:T(1,128)}, u32[]{:S(2)}) copy-start(f32[4,1,384]{2,1,0:T(1,128)} %param.5) | copy-start | bytes 18436
  0.6 19.5 %collective-permute-start.1 = (f32[4,640,256]{2,1,0:T(8,128)}, f32[4,640,256]{2,1,0:T(8,128)}, u32[]{:S(2)}, u32[]{:S(2)}) collective-permute-start(f32[4,640,256]{2,1,0:T(8,128)} %bitcast.12), channel_id=1, source_target_pairs={{0,4},{4,0},{1,5},{5,1},{2,6},{6,2},{3,7},{7,3},{8,12},{12,8},{9,1... | collective-permute-start | bytes 7864328 | tf_op jit(solution)/shard_map/ppermute | solution.py:503
  11.4 18.7 %all-to-all-start = ((f32[4,64,8,128]{3,2,1,0:T(8,128)}), f32[4,64,8,128]{3,2,1,0:T(8,128)S(1)}, u32[]{:S(2)}, u32[]{:S(2)}) async-start(f32[4,64,8,128]{3,2,1,0:T(8,128)} %pack.1), calls=%async_computation | async-start | bytes 2097152 | tf_op jit(solution)/shard_map/all_to_all | solution.py:506
  14.9 4.9 %collective-permute-start = (f32[4,384]{1,0:T(4,128)S(1)}, f32[4,384]{1,0:T(4,128)S(1)}, u32[]{:S(2)}, u32[]{:S(2)}) collective-permute-start(f32[4,384]{1,0:T(4,128)S(1)} %bitcast.16), channel_id=1, source_target_pairs={{0,4},{4,0},{1,5},{5,1},{2,6},{6,2},{3,7},{7,3},{8,12},{12,8},{9,1... | collective-permute-start | bytes 18440 | tf_op jit(solution)/shard_map/ppermute | solution.py:503
  77.0 14.9 %all-to-all-start.3 = ((f32[4,64,8,128]{3,2,1,0:T(8,128)}), f32[4,64,8,128]{3,2,1,0:T(8,128)S(1)}, u32[]{:S(2)}, u32[]{:S(2)}) async-start(f32[4,64,8,128]{3,2,1,0:T(8,128)} %copies.2), calls=%async_computation.3 | async-start | bytes 2097152 | tf_op jit(solution)/shard_map/all_to_all | solution.py:523
  80.5 8.7 %collective-permute-start.2 = (f32[2,4,64,256]{3,2,1,0:T(8,128)}, f32[2,4,64,256]{3,2,1,0:T(8,128)}, u32[]{:S(2)}, u32[]{:S(2)}) collective-permute-start(f32[2,4,64,256]{3,2,1,0:T(8,128)} %get-tuple-element.42.refs_8_.refs_9_), channel_id=1, source_target_pairs={{0,4},{4,0},{1,5},{5,1},{2,6},{6,2},{3,7},{7,3},{8,12},{12,8},{9,1... | collective-permute-start | bytes 1572872 | tf_op jit(solution)/shard_map/ppermute | solution.py:503
  135.1 14.5 %all-to-all-start.6 = ((f32[4,64,8,128]{3,2,1,0:T(8,128)}), f32[4,64,8,128]{3,2,1,0:T(8,128)S(1)}, u32[]{:S(2)}, u32[]{:S(2)}) async-start(f32[4,64,8,128]{3,2,1,0:T(8,128)} %copies.3), calls=%async_computation.6 | async-start | bytes 2097152 | tf_op jit(solution)/shard_map/all_to_all | solution.py:523
  138.6 9.2 %collective-permute-start.3 = (f32[2,4,64,256]{3,2,1,0:T(8,128)}, f32[2,4,64,256]{3,2,1,0:T(8,128)}, u32[]{:S(2)}, u32[]{:S(2)}) collective-permute-start(f32[2,4,64,256]{3,2,1,0:T(8,128)} %get-tuple-element.44.refs_8_.refs_10_), channel_id=1, source_target_pairs={{0,4},{4,0},{1,5},{5,1},{2,6},{6,2},{3,7},{7,3},{8,12},{12,8},{9,1... | collective-permute-start | bytes 1572872 | tf_op jit(solution)/shard_map/ppermute | solution.py:503
  171.9 17.2 %all-to-all-start.8 = ((f32[64,8,128]{2,1,0:T(8,128)}), f32[64,8,128]{2,1,0:T(8,128)S(1)}, u32[]{:S(2)}, u32[]{:S(2)}) async-start(f32[64,8,128]{2,1,0:T(8,128)} %shard_map.56), calls=%async_computation.8 | async-start | bytes 524288 | tf_op jit(solution)/shard_map/all_to_all | solution.py:519
  176.5 9.0 %collective-permute-start.4 = (f32[4,64,256]{2,1,0:T(8,128)}, f32[4,64,256]{2,1,0:T(8,128)S(1)}, u32[]{:S(2)}, u32[]{:S(2)}) collective-permute-start(f32[4,64,256]{2,1,0:T(8,128)} %get-tuple-element.46), channel_id=1, source_target_pairs={{0,4},{4,0},{1,5},{5,1},{2,6},{6,2},{3,7},{7,3},{8,12},{12,8},{9,1... | collective-permute-start | bytes 786440 | tf_op jit(solution)/shard_map/ppermute | solution.py:503
  185.6 0.9 copy-start
  189.1 9.9 %collective-permute-start.5 = (f32[64,8,128]{2,1,0:T(8,128)S(1)}, f32[64,8,128]{2,1,0:T(8,128)S(1)}, u32[]{:S(2)}, u32[]{:S(2)}) collective-permute-start(f32[64,8,128]{2,1,0:T(8,128)S(1)} %all-to-all-done.8.mine_ref), channel_id=1, source_target_pairs={{0,4},{4,0},{1,5},{5,1},{2,6},{6,2},{3,7},{7,3},{8,12},{12,8},{9,1... | collective-permute-start | bytes 786440 | tf_op jit(solution)/shard_map/ppermute | solution.py:503
